TPU v7x, 128 devices: a whole 4x4x4 slice. The times are simulated.
128 devices in a mesh: lang: 4 (over y), seq: 32 (over x, z, core).
Axes of the slice: x: 4, y: 4, z: 4, core: 2. Of those that a mesh axis runs over, the one named last changes fastest.
Arguments:
- q_stream: bfloat16 [4, 4096, 4096], P('lang', 'seq'), may hold values from -6 to 6
- k_stream: bfloat16 [4, 4096, 4096], P('lang', 'seq'), may hold values from -6 to 6
- v_stream: bfloat16 [4, 4096, 4096], P('lang', 'seq'), may hold values from -6 to 6
- lang_ids: int32 [4, 64], P('lang', 'seq'), may hold values from 0 to 15
- short_taps: bfloat16 [16, 3, 3, 4096], P('lang'), may hold values from -4 to 4
- adapter_down: bfloat16 [16, 16, 4096], P('lang'), may hold values from -0.09375 to 0.09375
- adapter_up: bfloat16 [16, 16, 4096], P('lang'), may hold values from -1.5 to 1.5
- long_filter: float32 [4096, 4096], P(None, 'seq'), as said below
- bypass_coefficient: float32 [4096], replicated, may hold values from 0.5 to 1.5
Outputs:
- output: bfloat16 [4, 4096, 4096], P('lang', 'seq')
Inputs may be any that keep to these rules, and one draw needn't show every extreme that they name: `long_filter`: each channel's filter may be rough in the lag.
All inputs are finite; a program needn't handle non-finite values.
Results may differ from a plain program's by a relative error of at most 0.009.
Values may be sent and summed in bfloat16 or wider, within the bound.
A program may use at most 128 MiB of HBM per device.

v0:
```python
import math

import jax
import jax.numpy as jnp
import ml_dtypes
import numpy as np
from jax import lax
from jax.experimental import pallas as pl
from jax.experimental.pallas import tpu as pltpu
from jax.sharding import PartitionSpec as P

LANES = 128
ROWS = 16


def shifted_2(x, axis, by):
    length = lax.axis_size(axis)
    pairs = [(i, i + by) for i in range(length) if 0 <= i + by < length]
    return lax.ppermute(x, axis, pairs)


def dft_tables():
    k1 = np.arange(512)[:, None]
    a = np.arange(512)[None, :]
    ang = 2.0 * np.pi * ((2 * k1 + 1) * a % 2048) / 2048.0
    table = np.concatenate([np.cos(ang), -np.sin(ang)], 0).astype(np.float32)
    one = 2.0 * np.pi * (2 * np.arange(512) + 1) / 16384.0
    step = np.stack([np.cos(one), -np.sin(one)]).astype(np.float32)
    step = np.ascontiguousarray(np.broadcast_to(step[:, :, None], (2, 512, LANES)))
    fwd = table.astype(ml_dtypes.bfloat16)
    return fwd, np.ascontiguousarray(fwd.T), step


def cadd(p, q):
    return p[0] + q[0], p[1] + q[1]


def csub(p, q):
    return p[0] - q[0], p[1] - q[1]


def cmul(p, q):
    return p[0] * q[0] - p[1] * q[1], p[0] * q[1] + p[1] * q[0]


def cmul_conj(p, q):
    return p[0] * q[0] + p[1] * q[1], p[1] * q[0] - p[0] * q[1]


def quarter(p, sign):
    return (p[1], -p[0]) if sign > 0 else (-p[1], p[0])


def dft4(z0, z1, z2, z3, sign):
    s0, s1 = cadd(z0, z2), csub(z0, z2)
    s2, s3 = cadd(z1, z3), quarter(csub(z1, z3), sign)
    return cadd(s0, s2), cadd(s1, s3), csub(s0, s2), csub(s1, s3)


def dft8(z, sign):
    half = math.sqrt(0.5)
    even = dft4(z[0], z[2], z[4], z[6], sign)
    odd = dft4(z[1], z[3], z[5], z[7], sign)
    o1, o3 = odd[1], odd[3]
    if sign > 0:
        o1 = ((o1[0] + o1[1]) * half, (o1[1] - o1[0]) * half)
        o3 = ((o3[1] - o3[0]) * half, (o3[0] + o3[1]) * -half)
    else:
        o1 = ((o1[0] - o1[1]) * half, (o1[0] + o1[1]) * half)
        o3 = ((o3[0] + o3[1]) * -half, (o3[0] - o3[1]) * half)
    turned = (odd[0], o1, quarter(odd[2], sign), o3)
    return [cadd(e, o) for e, o in zip(even, turned)] + [csub(e, o) for e, o in zip(even, turned)]


def lane(b):
    return slice(b * LANES, (b + 1) * LANES)


def stage_matmul(out_ref, left_ref, right_refs, width=256):
    columns = out_ref.shape[1]

    @pl.loop(0, columns // width)
    def _(j):
        cols = pl.ds(pl.multiple_of(j * width, width), width)
        total = None
        for right_ref in right_refs:
            term = jnp.dot(left_ref[...], right_ref[:, cols], preferred_element_type=jnp.float32)
            total = term if total is None else total + term
        out_ref[:, cols] = total


def load_points(p_ref, rows_re, rows_im):
    return [(p_ref[rows_re, lane(b)], p_ref[rows_im, lane(b)]) for b in range(8)]


def filter_spectrum(filt_ref, table_ref, step_ref, high_ref, low_ref, p_ref, h_ref, tw_ref):
    for b in range(8):
        @pl.loop(0, 4)
        def _(i):
            rows = filt_ref[pl.ds(i * 1024 + b, 128, stride=8), :]
            high = rows.astype(jnp.bfloat16)
            at = pl.ds(pl.multiple_of(i * 128, 128), 128)
            high_ref[at, lane(b)] = high
            low_ref[at, lane(b)] = (rows - high.astype(jnp.float32)).astype(jnp.bfloat16)
    stage_matmul(p_ref, table_ref, [high_ref, low_ref])

    @pl.loop(0, 512 // ROWS)
    def _(i):
        re = pl.ds(pl.multiple_of(i * ROWS, ROWS), ROWS)
        im = pl.ds(pl.multiple_of(512 + i * ROWS, ROWS), ROWS)
        points = load_points(p_ref, re, im)
        step = (step_ref[0, re, :], step_ref[1, re, :])
        turn = step
        for b in range(1, 8):
            tw_ref[re, lane(b)] = turn[0]
            tw_ref[im, lane(b)] = turn[1]
            points[b] = cmul(points[b], turn)
            if b < 7:
                turn = cmul(turn, step)
        for k2, value in enumerate(dft8(points, 1)):
            h_ref[re, lane(k2)] = value[0] * (2.0 / 8192.0)
            h_ref[im, lane(k2)] = value[1] * (2.0 / 8192.0)


def spectrum_product(p_ref, h_ref, tw_ref, g_ref):
    @pl.loop(0, 512 // ROWS)
    def _(i):
        re = pl.ds(pl.multiple_of(i * ROWS, ROWS), ROWS)
        im = pl.ds(pl.multiple_of(512 + i * ROWS, ROWS), ROWS)
        points = load_points(p_ref, re, im)
        for b in range(1, 8):
            points[b] = cmul(points[b], (tw_ref[re, lane(b)], tw_ref[im, lane(b)]))
        spec = dft8(points, 1)
        spec = [cmul(v, (h_ref[re, lane(k)], h_ref[im, lane(k)])) for k, v in enumerate(spec)]
        back = dft8(spec, -1)
        for b in range(8):
            value = back[b]
            if b > 0:
                value = cmul_conj(value, (tw_ref[re, lane(b)], tw_ref[im, lane(b)]))
            g_ref[re, lane(b)] = value[0].astype(jnp.bfloat16)
            g_ref[im, lane(b)] = value[1].astype(jnp.bfloat16)


def conv_kernel(sig_ref, filt_ref, skip_ref, table_ref, back_ref, step_ref, out_ref, high, low, p, h, tw, g):
    filter_spectrum(filt_ref, table_ref, step_ref, high, low, p, h, tw)
    stage_matmul(p, table_ref, [sig_ref])
    spectrum_product(p, h, tw, g)
    stage_matmul(p.at[0:512], back_ref, [g])
    for b in range(8):
        out_ref[:, lane(b)] = (
            p[0:512, lane(b)] + skip_ref[...] * sig_ref[:, lane(b)].astype(jnp.float32)
        ).astype(jnp.bfloat16)


def long_mix(signal, filt, skip_cols):
    fwd, back, step = dft_tables()
    sig = signal.reshape(512, 8 * LANES)
    out = pl.pallas_call(
        conv_kernel,
        out_shape=jax.ShapeDtypeStruct((512, 8 * LANES), jnp.bfloat16),
        in_specs=[pl.BlockSpec(memory_space=pltpu.VMEM)] * 6,
        out_specs=pl.BlockSpec(memory_space=pltpu.VMEM),
        scratch_shapes=[
            pltpu.VMEM((512, 1024), jnp.bfloat16),
            pltpu.VMEM((512, 1024), jnp.bfloat16),
            pltpu.VMEM((1024, 1024), jnp.float32),
            pltpu.VMEM((1024, 1024), jnp.float32),
            pltpu.VMEM((1024, 1024), jnp.float32),
            pltpu.VMEM((1024, 1024), jnp.bfloat16),
        ],
        compiler_params=pltpu.CompilerParams(vmem_limit_bytes=56 << 20),
    )(sig, filt, skip_cols[None, :], jnp.asarray(fwd), jnp.asarray(back), jnp.asarray(step))
    return out.reshape(signal.shape)


def short_filter(stream, rim_rows, taps_mine, stream_index, seg_count):
    token_rows, model_channel_width = stream.shape
    seg_len = token_rows // seg_count
    extended = jnp.concatenate([rim_rows, stream], 0)
    summed = jnp.zeros((seg_count, seg_len, model_channel_width), jnp.float32)
    for offset in range(3):
        shifted = extended[2 - offset : 2 - offset + token_rows].reshape(
            seg_count, seg_len, model_channel_width
        )
        summed = summed + shifted.astype(jnp.float32) * taps_mine[:, offset, stream_index, :][
            :, None, :
        ].astype(jnp.float32)
    return summed


def local(
    q_stream,
    k_stream,
    v_stream,
    lang_ids,
    short_taps,
    adapter_down,
    adapter_up,
    long_filter,
    bypass_coefficient,
):
    q_rows, k_rows, v_rows = (q_stream[0], k_stream[0], v_stream[0])
    token_rows, model_channel_width = q_rows.shape
    seg_count = lang_ids.shape[1]
    my_langs = lang_ids[0]
    lang_dev = short_taps.shape[0]
    groups = lax.axis_size("lang")
    wanted = lax.all_gather(my_langs, "lang", axis=0, tiled=True)
    local_ids = wanted - lax.axis_index("lang") * lang_dev
    table = (local_ids[:, None] == jnp.arange(lang_dev, dtype=jnp.int32)[None, :]).astype(
        jnp.bfloat16
    )
    send_down = jnp.einsum(
        "sl,lrd->srd", table, adapter_down, preferred_element_type=jnp.float32
    ).astype(jnp.bfloat16)
    send_up = jnp.einsum(
        "sl,lrd->srd", table, adapter_up, preferred_element_type=jnp.float32
    ).astype(jnp.bfloat16)
    send_taps = jnp.einsum(
        "sl,ljkd->sjkd", table, short_taps, preferred_element_type=jnp.float32
    ).astype(jnp.bfloat16)
    got_down, got_up, got_taps = (
        lax.all_to_all(
            send_down.reshape((groups, seg_count) + send_down.shape[1:]),
            "lang",
            split_axis=0,
            concat_axis=0,
            tiled=True,
        ),
        lax.all_to_all(
            send_up.reshape((groups, seg_count) + send_up.shape[1:]),
            "lang",
            split_axis=0,
            concat_axis=0,
            tiled=True,
        ),
        lax.all_to_all(
            send_taps.reshape((groups, seg_count) + send_taps.shape[1:]),
            "lang",
            split_axis=0,
            concat_axis=0,
            tiled=True,
        ),
    )
    down_mine = jnp.sum(got_down.astype(jnp.float32), axis=0).astype(jnp.bfloat16)
    up_mine = jnp.sum(got_up.astype(jnp.float32), axis=0).astype(jnp.bfloat16)
    taps_mine = jnp.sum(got_taps.astype(jnp.float32), axis=0).astype(jnp.bfloat16)
    rims = shifted_2(jnp.stack([q_rows[-2:], k_rows[-2:], v_rows[-2:]]), "seq", 1)
    qshort = short_filter(q_rows, rims[0], taps_mine, 0, seg_count).astype(jnp.bfloat16)
    query_local_smoothed = short_filter(k_rows, rims[1], taps_mine, 1, seg_count)
    payload_local_smoothed = short_filter(v_rows, rims[2], taps_mine, 2, seg_count)
    modulating_cosine = (
        (query_local_smoothed * payload_local_smoothed)
        .astype(jnp.bfloat16)
        .reshape(token_rows, model_channel_width)
    )
    low = jnp.einsum("snd,srd->snr", qshort, down_mine, preferred_element_type=jnp.float32).astype(
        jnp.bfloat16
    )
    gate = qshort.astype(jnp.float32) + jnp.einsum(
        "snr,srd->snd", low, up_mine, preferred_element_type=jnp.float32
    )
    gate = gate.reshape(token_rows, model_channel_width)
    seq_devs = lax.axis_size("seq")
    per_seq = model_channel_width // seq_devs
    seq_place = lax.axis_index("seq")
    feature_indices = lax.all_to_all(
        modulating_cosine, "seq", split_axis=1, concat_axis=0, tiled=True
    )
    skip_cols = lax.dynamic_slice_in_dim(bypass_coefficient, seq_place * per_seq, per_seq, 0)
    gated_combination = long_mix(feature_indices, long_filter, skip_cols)
    back = lax.all_to_all(gated_combination, "seq", split_axis=0, concat_axis=1, tiled=True)
    return (gate * back.astype(jnp.float32)).astype(jnp.bfloat16)[None]


def solution(mesh):
    placed = (
        P("lang", "seq", None),
        P("lang", "seq", None),
        P("lang", "seq", None),
        P("lang", "seq"),
        P("lang", None, None, None),
        P("lang", None, None),
        P("lang", None, None),
        P(None, "seq"),
        P(),
    )
    return jax.shard_map(
        local, mesh=mesh, in_specs=placed, out_specs=P("lang", "seq", None), check_vma=False
    )
```

profile of v0, /device:TPU:1, one launch (start us, length us, event | category | flops | bytes accessed | tf_op | source)
XLA Modules:
  0.0 132.2 jit_solution(5129218552201580880)
XLA Ops:
  0.0 0.9 slice.68
  0.9 0.9 slice.69
  1.8 0.9 slice.67
  2.7 0.1 pad_maximum_fusion.3
  2.7 4.9 %collective-permute-start = (bf16[3,2,4096]{2,1,0:T(2,128)(2,1)S(1)}, bf16[3,2,4096]{2,1,0:T(2,128)(2,1)S(1)}, u32[]{:S(2)}, u32[]{:S(2)}) collective-permute-start(bf16[3,2,4096]{2,1,0:T(2,128)(2,1)S(1)} %pad_maximum_fusion.3), channel_id=1, source_target_pairs={{0,1},{1,2},{2,3},{3,4},{4,5},{5,6},{6,7},{7,8},{8,9},{9,10},{10,1... | collective-permute-start | bytes 147464 | tf_op jit(solution)/shard_map/ppermute | solution.py:19
  7.7 1.2 dynamic-slice
  9.6 0.8 bitcast_dynamic-update-slice_fusion
  10.4 7.3 %all-reduce = s32[8]{0:T(128)S(1)} all-reduce(s32[8]{0:T(128)S(1)} %bitcast_dynamic-update-slice_fusion), channel_id=2, replica_groups=mesh['lang'=4,'seq'=32] {'lang'}, use_global_device_ids=true, to_apply=%add | all-reduce | flops 8 | bytes 64
  17.7 1.3 %convolution_convert_fusion.2 = bf16[8,3,3,4096]{3,0,2,1:T(8,128)(2,1)S(1)} fusion(bf16[4,3,3,4096]{3,0,2,1:T(4,128)(2,1)} %param.16, s32[8]{0:T(128)S(1)} %broadcast_subtract_fusion), kind=kOutput, calls=%fused_computation.3 | convolution fusion | flops 2654240 | bytes 884768 | tf_op jit(solution)/shard_map/sl,ljkd->sjkd/dot_general | solution.py:219
  19.0 0.4 reshape.158
  19.4 1.4 %copy.17 = bf16[4,2,3,3,4096]{4,1,3,2,0:T(2,128)(2,1)} copy(bf16[4,2,3,3,4096]{4,1,0,3,2:T(2,128)(2,1)S(1)} %reshape.158) | data formatting | bytes 1179648 | tf_op jit(solution)/shard_map/reshape | solution.py:238
  20.8 3.5 %all-to-all-start = ((bf16[4,2,3,3,4096]{4,1,3,2,0:T(2,128)(2,1)}), bf16[4,2,3,3,4096]{4,1,3,2,0:T(2,128)(2,1)S(1)}, u32[]{:S(2)}, u32[]{:S(2)}) async-start(bf16[4,2,3,3,4096]{4,1,3,2,0:T(2,128)(2,1)} %copy.17), calls=%async_computation | async-start | bytes 1179648 | tf_op jit(solution)/shard_map/all_to_all | solution.py:237
  24.3 0.6 convolution_convert_fusion.1
  24.9 0.7 reshape.159
  25.6 2.1 %copy.19 = bf16[4,2,16,4096]{3,1,2,0:T(2,128)(2,1)} copy(bf16[4,2,16,4096]{3,1,0,2:T(2,128)(2,1)S(1)} %reshape.159) | data formatting | bytes 2097152 | tf_op jit(solution)/shard_map/reshape | solution.py:224
  27.7 0.0 collective-permute-done
  27.7 6.8 %all-to-all-done = bf16[4,2,3,3,4096]{4,1,3,2,0:T(2,128)(2,1)S(1)} async-done(((bf16[4,2,3,3,4096]{4,1,3,2,0:T(2,128)(2,1)}), bf16[4,2,3,3,4096]{4,1,3,2,0:T(2,128)(2,1)S(1)}, u32[]{:S(2)}, u32[]{:S(2)}) %all-to-all-start) | async-done | bytes 589856 | tf_op jit(solution)/shard_map/all_to_all | solution.py:237
  34.5 3.5 %all-to-all-start.1 = ((bf16[4,2,16,4096]{3,1,2,0:T(2,128)(2,1)}), bf16[4,2,16,4096]{3,1,2,0:T(2,128)(2,1)S(1)}, u32[]{:S(2)}, u32[]{:S(2)}) async-start(bf16[4,2,16,4096]{3,1,2,0:T(2,128)(2,1)} %copy.19), calls=%async_computation.1 | async-start | bytes 2097152 | tf_op jit(solution)/shard_map/all_to_all | solution.py:223
  38.0 0.8 reduce_sum.36
  38.8 0.1 fusion.34
  38.9 0.0 copy-done.3
  39.0 3.3 %fusion.5 = bf16[128,4096]{1,0:T(8,128)(2,1)S(1)} fusion(bf16[128,4096]{1,0:T(8,128)(2,1)S(1)} %bitcast.132, bf16[128,4096]{1,0:T(8,128)(2,1)} %bitcast.133, bf16[2,4096]{1,0:T(2,128)(2,1)S(1)} %get-tuple-element.17, bf16[2,4096]{1,0:T(2,128)(2,1)S(1)} %get-tuple-element.18, f32[2,4096]{1,0:T(2,128)S(1)} %get-tuple-element.8, ...), kind=kLoop, calls=%fused_computation.13 | loop fusion | flops 15728640 | bytes 3375104 | tf_op jit(solution)/shard_map/convert_element_type | solution.py:254
  42.2 0.0 copy-start.4
  42.2 1.3 copy_bitcast_fusion
  43.5 8.8 %all-to-all-done.1 = bf16[4,2,16,4096]{3,1,2,0:T(2,128)(2,1)S(1)} async-done(((bf16[4,2,16,4096]{3,1,2,0:T(2,128)(2,1)}), bf16[4,2,16,4096]{3,1,2,0:T(2,128)(2,1)S(1)}, u32[]{:S(2)}, u32[]{:S(2)}) %all-to-all-start.1) | async-done | bytes 1048608 | tf_op jit(solution)/shard_map/all_to_all | solution.py:223
  52.3 8.0 %all-to-all-start.3 = ((bf16[128,32,128]{2,0,1:T(8,128)(2,1)}), bf16[128,32,128]{2,0,1:T(8,128)(2,1)S(1)}, u32[]{:S(2)}, u32[]{:S(2)}) async-start(bf16[128,32,128]{2,0,1:T(8,128)(2,1)} %copy_bitcast_fusion), calls=%async_computation.3 | async-start | bytes 2097152 | tf_op jit(solution)/shard_map/all_to_all | solution.py:267
  60.4 1.6 %convolution_convert_fusion = bf16[8,16,4096]{2,0,1:T(8,128)(2,1)} fusion(bf16[4,16,4096]{2,1,0:T(8,128)(2,1)S(1)} %copy-done.4, s32[8]{0:T(128)S(1)} %broadcast_subtract_fusion), kind=kOutput, calls=%fused_computation.1 | convolution fusion | flops 4718624 | bytes 1572896 | tf_op jit(solution)/shard_map/sl,lrd->srd/dot_general | solution.py:216
  61.9 2.5 %reshape.160 = bf16[4,2,16,4096]{3,1,0,2:T(2,128)(2,1)} reshape(bf16[8,16,4096]{2,0,1:T(8,128)(2,1)} %convolution_convert_fusion) | data formatting | bytes 2097152 | tf_op jit(solution)/shard_map/reshape | solution.py:231
  64.5 3.3 %copy.22 = bf16[4,2,16,4096]{3,1,2,0:T(2,128)(2,1)} copy(bf16[4,2,16,4096]{3,1,0,2:T(2,128)(2,1)} %reshape.160) | data formatting | bytes 2097152 | tf_op jit(solution)/shard_map/reshape | solution.py:231
  67.8 9.5 %all-to-all-done.3 = bf16[128,32,128]{2,0,1:T(8,128)(2,1)S(1)} async-done(((bf16[128,32,128]{2,0,1:T(8,128)(2,1)}), bf16[128,32,128]{2,0,1:T(8,128)(2,1)S(1)}, u32[]{:S(2)}, u32[]{:S(2)}) %all-to-all-start.3) | async-done | bytes 1048608 | tf_op jit(solution)/shard_map/all_to_all | solution.py:267
  77.3 1.0 copy-done.2
  78.3 3.5 %all-to-all-start.2 = ((bf16[4,2,16,4096]{3,1,2,0:T(2,128)(2,1)}), bf16[4,2,16,4096]{3,1,2,0:T(2,128)(2,1)S(1)}, u32[]{:S(2)}, u32[]{:S(2)}) async-start(bf16[4,2,16,4096]{3,1,2,0:T(2,128)(2,1)} %copy.22), calls=%async_computation.2 | async-start | bytes 2097152 | tf_op jit(solution)/shard_map/all_to_all | solution.py:230
  81.8 1.3 %dynamic-slice_bitcast_fusion.skip_ref = f32[1,128]{1,0:T(1,128)} fusion(f32[4096]{0:T(1024)} %param.20, s32[]{:T(128)S(6)} %select_n.3), kind=kLoop, calls=%fused_computation.75 | loop fusion | bytes 1028 | tf_op jit(solution)/shard_map/broadcast_in_dim | solution.py:172
  83.1 2.3 %reshape.162.sig_ref = bf16[512,1024]{1,0:T(8,128)(2,1)} reshape(bf16[32,128,128]{2,1,0:T(8,128)(2,1)} %bitcast.130) | data formatting | bytes 2097152 | tf_op jit(solution)/shard_map/reshape | solution.py:157
  85.4 15.3 %shard_map.118 = bf16[512,1024]{1,0:T(8,128)(2,1)} custom-call(bf16[512,1024]{1,0:T(8,128)(2,1)} %reshape.162.sig_ref, f32[4096,128]{1,0:T(8,128)} %filt_ref.1, f32[1,128]{1,0:T(1,128)} %dynamic-slice_bitcast_fusion.skip_ref, bf16[1024,512]{1,0:T(8,128)(2,1)} %constant.28.clone.table_ref, bf16[512,1024]{1,0:T(8,128)(2,1)} %constant.29.clone.back_ref, ...), custom_call_target="tpu_custom_call" | custom-call | tf_op jit(solution)/shard_map/pallas_call | solution.py:158
  100.8 2.3 %all_to_all.37 = bf16[32,128,128]{2,1,0:T(8,128)(2,1)} reshape(bf16[512,1024]{1,0:T(8,128)(2,1)} %shard_map.118) | data formatting | bytes 2097152 | tf_op jit(solution)/shard_map/all_to_all | solution.py:272
  103.1 0.0 all-to-all-done.2
  103.1 1.0 copy-done.1
  104.0 4.0 %all-to-all-start.4 = ((bf16[32,128,128]{2,1,0:T(8,128)(2,1)}), bf16[32,128,128]{2,1,0:T(8,128)(2,1)S(1)}, u32[]{:S(2)}, u32[]{:S(2)}) async-start(bf16[32,128,128]{2,1,0:T(8,128)(2,1)} %all_to_all.37), calls=%async_computation.4 | async-start | bytes 2097152 | tf_op jit(solution)/shard_map/all_to_all | solution.py:272
  108.0 3.4 %fusion.12 = (bf16[128,4096]{1,0:T(8,128)(2,1)}, bf16[128,4096]{1,0:T(8,128)(2,1)}) fusion(bf16[2,4096]{1,0:T(2,128)(2,1)S(1)} %get-tuple-element.16, bf16[128,4096]{1,0:T(8,128)(2,1)} %bitcast.134), kind=kLoop, calls=%fused_computation.34 | loop fusion | flops 4194304 | bytes 3162112 | tf_op jit(solution)/shard_map/concatenate | solution.py:179
  111.4 1.5 %reduce_sum.37 = bf16[2,16,4096]{2,0,1:T(2,128)(2,1)S(1)} reduce(bf16[4,2,16,4096]{3,1,2,0:T(2,128)(2,1)S(1)} %all-to-all-done.1, bf16[]{:T(256)} %constant.23.clone.1), dimensions={0}, to_apply=%region_1.0 | reduce | flops 393216 | bytes 1310722 | tf_op jit(solution)/shard_map/reduce_sum | solution.py:245
  112.9 2.7 %reduce_sum.38 = bf16[2,16,4096]{2,0,1:T(2,128)(2,1)S(1)} reduce(bf16[4,2,16,4096]{3,1,2,0:T(2,128)(2,1)} %copy-done.1, bf16[]{:T(256)} %constant.23.clone.1), dimensions={0}, to_apply=%region_2.0 | reduce | flops 393216 | bytes 1310722 | tf_op jit(solution)/shard_map/reduce_sum | solution.py:246
  115.6 6.0 %convolution_add_fusion = f32[2,64,4096]{2,1,0:T(8,128)} fusion(bf16[2,64,4096]{2,1,0:T(8,128)(2,1)} %bitcast.137, bf16[2,64,4096]{2,1,0:T(8,128)(2,1)} %bitcast.136, bf16[2,64,4096]{2,1,0:T(8,128)(2,1)} %bitcast.135, f32[2,4096]{1,0:T(2,128)S(1)} %get-tuple-element.14, f32[2,4096]{1,0:T(2,128)S(1)} %get-tuple-element.15, f32[2,4096]{1,0:T(2,128)S(1)} %get-tuple-element.7, ...), kind=kOutput, calls=%fused_computation | convolution fusion | flops 44042240 | bytes 5865472 | tf_op jit(solution)/shard_map/snr,srd->snd/dot_general | solution.py:260
  121.6 3.3 %all-to-all-done.4 = bf16[32,128,128]{2,1,0:T(8,128)(2,1)S(1)} async-done(((bf16[32,128,128]{2,1,0:T(8,128)(2,1)}), bf16[32,128,128]{2,1,0:T(8,128)(2,1)S(1)}, u32[]{:S(2)}, u32[]{:S(2)}) %all-to-all-start.4) | async-done | bytes 1048608 | tf_op jit(solution)/shard_map/all_to_all | solution.py:272
  124.9 0.2 convert_bitcast_fusion
  125.2 2.5 %copy.26 = f32[128,32,128]{2,1,0:T(8,128)} copy(f32[128,32,128]{2,0,1:T(8,128)S(1)} %convert_bitcast_fusion) | data formatting | bytes 4194304 | tf_op jit(solution)/shard_map/convert_element_type | solution.py:273
  127.7 1.7 %reshape.175 = f32[1,128,4096]{2,1,0:T(8,128)S(1)} reshape(f32[128,32,128]{2,1,0:T(8,128)} %copy.26) | data formatting | bytes 4194304 | tf_op jit(solution)/shard_map/convert_element_type | solution.py:273
  129.4 2.8 %fusion.9 = bf16[1,128,4096]{2,1,0:T(8,128)(2,1)} fusion(f32[1,128,4096]{2,1,0:T(8,128)S(1)} %reshape.175, f32[1,128,4096]{2,1,0:T(8,128)} %bitcast.131), kind=kLoop, calls=%fused_computation.23 | loop fusion | flops 1048576 | bytes 5242880 | tf_op jit(solution)/shard_map/convert_element_type | solution.py:273
  (9 shorter events, 0.1 us)
Async XLA Ops:
  0.0 24.2 %copy-start = (bf16[4,16,4096]{2,1,0:T(8,128)(2,1)S(1)}, bf16[4,16,4096]{2,1,0:T(8,128)(2,1)}, u32[]{:S(2)}) copy-start(bf16[4,16,4096]{2,1,0:T(8,128)(2,1)} %param.17) | copy-start | bytes 1572868
  2.7 24.9 %collective-permute-start = (bf16[3,2,4096]{2,1,0:T(2,128)(2,1)S(1)}, bf16[3,2,4096]{2,1,0:T(2,128)(2,1)S(1)}, u32[]{:S(2)}, u32[]{:S(2)}) collective-permute-start(bf16[3,2,4096]{2,1,0:T(2,128)(2,1)S(1)} %pad_maximum_fusion.3), channel_id=1, source_target_pairs={{0,1},{1,2},{2,3},{3,4},{4,5},{5,6},{6,7},{7,8},{8,9},{9,10},{10,1... | collective-permute-start | bytes 147464 | tf_op jit(solution)/shard_map/ppermute | solution.py:19
  20.8 13.8 %all-to-all-start = ((bf16[4,2,3,3,4096]{4,1,3,2,0:T(2,128)(2,1)}), bf16[4,2,3,3,4096]{4,1,3,2,0:T(2,128)(2,1)S(1)}, u32[]{:S(2)}, u32[]{:S(2)}) async-start(bf16[4,2,3,3,4096]{4,1,3,2,0:T(2,128)(2,1)} %copy.17), calls=%async_computation | async-start | bytes 1179648 | tf_op jit(solution)/shard_map/all_to_all | solution.py:237
  27.7 11.3 %copy-start.3 = (bf16[1,128,4096]{2,1,0:T(8,128)(2,1)S(1)}, bf16[1,128,4096]{2,1,0:T(8,128)(2,1)}, u32[]{:S(2)}) copy-start(bf16[1,128,4096]{2,1,0:T(8,128)(2,1)} %param.14) | copy-start | bytes 3145732
  34.5 17.8 %all-to-all-start.1 = ((bf16[4,2,16,4096]{3,1,2,0:T(2,128)(2,1)}), bf16[4,2,16,4096]{3,1,2,0:T(2,128)(2,1)S(1)}, u32[]{:S(2)}, u32[]{:S(2)}) async-start(bf16[4,2,16,4096]{3,1,2,0:T(2,128)(2,1)} %copy.19), calls=%async_computation.1 | async-start | bytes 2097152 | tf_op jit(solution)/shard_map/all_to_all | solution.py:223
  42.2 18.1 %copy-start.4 = (bf16[4,16,4096]{2,1,0:T(8,128)(2,1)S(1)}, bf16[4,16,4096]{2,1,0:T(8,128)(2,1)}, u32[]{:S(2)}) copy-start(bf16[4,16,4096]{2,1,0:T(8,128)(2,1)} %param.18) | copy-start | bytes 1572868
  52.3 24.9 %all-to-all-start.3 = ((bf16[128,32,128]{2,0,1:T(8,128)(2,1)}), bf16[128,32,128]{2,0,1:T(8,128)(2,1)S(1)}, u32[]{:S(2)}, u32[]{:S(2)}) async-start(bf16[128,32,128]{2,0,1:T(8,128)(2,1)} %copy_bitcast_fusion), calls=%async_computation.3 | async-start | bytes 2097152 | tf_op jit(solution)/shard_map/all_to_all | solution.py:267
  77.3 1.0 copy-start.2
  78.3 24.8 %all-to-all-start.2 = ((bf16[4,2,16,4096]{3,1,2,0:T(2,128)(2,1)}), bf16[4,2,16,4096]{3,1,2,0:T(2,128)(2,1)S(1)}, u32[]{:S(2)}, u32[]{:S(2)}) async-start(bf16[4,2,16,4096]{3,1,2,0:T(2,128)(2,1)} %copy.22), calls=%async_computation.2 | async-start | bytes 2097152 | tf_op jit(solution)/shard_map/all_to_all | solution.py:230
  103.1 1.0 copy-start.1
  104.0 20.9 %all-to-all-start.4 = ((bf16[32,128,128]{2,1,0:T(8,128)(2,1)}), bf16[32,128,128]{2,1,0:T(8,128)(2,1)S(1)}, u32[]{:S(2)}, u32[]{:S(2)}) async-start(bf16[32,128,128]{2,1,0:T(8,128)(2,1)} %all_to_all.37), calls=%async_computation.4 | async-start | bytes 2097152 | tf_op jit(solution)/shard_map/all_to_all | solution.py:272
where the time goes:
time: 133 us; the launch traced here: 132 us
  local copies, waits for them, and re-layouts  28.5 us (21%)
  waiting for transfers between devices  28.5 us (21%)
  starting transfers between devices  27.4 us (21%)
  Pallas kernels  15.3 us (12%)
  other arithmetic  14.8 us (11%)
  matrix products  9.48 us (7%)
  blocking collectives  7.32 us (6%)
    pallas_call x1, Pallas kernels, long_mix(): pl.pallas_call(conv_kernel, out_shape=jax.ShapeDtypeStruct((512, 8 * LANE...  15.3 us
    all_to_all x1, waiting for transfers between devices, local(): lax.all_to_all(modulating_cosine, 'seq', split_axis=1, concat_axis=0, til...  9.5 us
    all_to_all x1, waiting for transfers between devices, local(): lax.all_to_all(send_down.reshape((groups, seg_count) + send_down.shape[1:...  8.84 us
    all_to_all x1, starting transfers between devices, local(): lax.all_to_all(modulating_cosine, 'seq', split_axis=1, concat_axis=0, til...  8.02 us
    unnamed x1, blocking collectives  7.32 us
    all_to_all x1, waiting for transfers between devices, local(): lax.all_to_all(send_taps.reshape((groups, seg_count) + send_taps.shape[1:...  6.82 us
    dot_general x1, matrix products, local(): jnp.einsum('snr,srd->snd', low, up_mine, preferred_element_type=jnp.float32)  5.99 us
    reshape x2, local copies, waits for them, and re-layouts, local(): send_up.reshape((groups, seg_count) + send_up.shape[1:])  5.84 us
  transfers between devices with their start and end apart: 6, of which 4 were waited for; matrix products, arithmetic and copies ran while one was open for 29% of the time, Pallas kernels for 12%

commit v1 on v0

v1 whole, which is shorter than its diff:
```python
import math

import jax
import jax.numpy as jnp
import ml_dtypes
import numpy as np
from jax import lax
from jax.experimental import pallas as pl
from jax.experimental.pallas import tpu as pltpu
from jax.sharding import PartitionSpec as P

LANES = 128
ROWS = 16


def dft_tables():
    k1 = np.arange(512)[:, None]
    a = np.arange(512)[None, :]
    ang = 2.0 * np.pi * ((2 * k1 + 1) * a % 2048) / 2048.0
    table = np.concatenate([np.cos(ang), -np.sin(ang)], 0).astype(np.float32)
    one = 2.0 * np.pi * (2 * np.arange(512) + 1) / 16384.0
    step = np.stack([np.cos(one), -np.sin(one)]).astype(np.float32)
    step = np.ascontiguousarray(np.broadcast_to(step[:, :, None], (2, 512, LANES)))
    fwd = table.astype(ml_dtypes.bfloat16)
    return fwd, np.ascontiguousarray(fwd.T), step


def cadd(p, q):
    return p[0] + q[0], p[1] + q[1]


def csub(p, q):
    return p[0] - q[0], p[1] - q[1]


def cmul(p, q):
    return p[0] * q[0] - p[1] * q[1], p[0] * q[1] + p[1] * q[0]


def cmul_conj(p, q):
    return p[0] * q[0] + p[1] * q[1], p[1] * q[0] - p[0] * q[1]


def quarter(p, sign):
    return (p[1], -p[0]) if sign > 0 else (-p[1], p[0])


def dft4(z0, z1, z2, z3, sign):
    s0, s1 = cadd(z0, z2), csub(z0, z2)
    s2, s3 = cadd(z1, z3), quarter(csub(z1, z3), sign)
    return cadd(s0, s2), cadd(s1, s3), csub(s0, s2), csub(s1, s3)


def dft8(z, sign):
    half = math.sqrt(0.5)
    even = dft4(z[0], z[2], z[4], z[6], sign)
    odd = dft4(z[1], z[3], z[5], z[7], sign)
    o1, o3 = odd[1], odd[3]
    if sign > 0:
        o1 = ((o1[0] + o1[1]) * half, (o1[1] - o1[0]) * half)
        o3 = ((o3[1] - o3[0]) * half, (o3[0] + o3[1]) * -half)
    else:
        o1 = ((o1[0] - o1[1]) * half, (o1[0] + o1[1]) * half)
        o3 = ((o3[0] + o3[1]) * -half, (o3[0] - o3[1]) * half)
    turned = (odd[0], o1, quarter(odd[2], sign), o3)
    return [cadd(e, o) for e, o in zip(even, turned)] + [csub(e, o) for e, o in zip(even, turned)]


def lane(b):
    return slice(b * LANES, (b + 1) * LANES)


def stage_matmul(out_ref, left_ref, right_refs, width=256):
    columns = out_ref.shape[1]

    @pl.loop(0, columns // width)
    def _(j):
        cols = pl.ds(pl.multiple_of(j * width, width), width)
        total = None
        for right_ref in right_refs:
            term = jnp.dot(left_ref[...], right_ref[:, cols], preferred_element_type=jnp.float32)
            total = term if total is None else total + term
        out_ref[:, cols] = total


def load_points(p_ref, rows_re, rows_im):
    return [(p_ref[rows_re, lane(b)], p_ref[rows_im, lane(b)]) for b in range(8)]


def filter_spectrum(filt_ref, table_ref, step_ref, high_ref, low_ref, p_ref, h_ref, tw_ref):
    for b in range(8):
        @pl.loop(0, 4)
        def _(i):
            rows = filt_ref[pl.ds(i * 1024 + b, 128, stride=8), :]
            high = rows.astype(jnp.bfloat16)
            at = pl.ds(pl.multiple_of(i * 128, 128), 128)
            high_ref[at, lane(b)] = high
            low_ref[at, lane(b)] = (rows - high.astype(jnp.float32)).astype(jnp.bfloat16)
    stage_matmul(p_ref, table_ref, [high_ref, low_ref])

    @pl.loop(0, 512 // ROWS)
    def _(i):
        re = pl.ds(pl.multiple_of(i * ROWS, ROWS), ROWS)
        im = pl.ds(pl.multiple_of(512 + i * ROWS, ROWS), ROWS)
        points = load_points(p_ref, re, im)
        step = (step_ref[0, re, :], step_ref[1, re, :])
        turn = step
        for b in range(1, 8):
            tw_ref[re, lane(b)] = turn[0]
            tw_ref[im, lane(b)] = turn[1]
            points[b] = cmul(points[b], turn)
            if b < 7:
                turn = cmul(turn, step)
        for k2, value in enumerate(dft8(points, 1)):
            h_ref[re, lane(k2)] = value[0] * (2.0 / 8192.0)
            h_ref[im, lane(k2)] = value[1] * (2.0 / 8192.0)


def spectrum_product(p_ref, h_ref, tw_ref, g_ref):
    @pl.loop(0, 512 // ROWS)
    def _(i):
        re = pl.ds(pl.multiple_of(i * ROWS, ROWS), ROWS)
        im = pl.ds(pl.multiple_of(512 + i * ROWS, ROWS), ROWS)
        points = load_points(p_ref, re, im)
        for b in range(1, 8):
            points[b] = cmul(points[b], (tw_ref[re, lane(b)], tw_ref[im, lane(b)]))
        spec = dft8(points, 1)
        spec = [cmul(v, (h_ref[re, lane(k)], h_ref[im, lane(k)])) for k, v in enumerate(spec)]
        back = dft8(spec, -1)
        for b in range(8):
            value = back[b]
            if b > 0:
                value = cmul_conj(value, (tw_ref[re, lane(b)], tw_ref[im, lane(b)]))
            g_ref[re, lane(b)] = value[0].astype(jnp.bfloat16)
            g_ref[im, lane(b)] = value[1].astype(jnp.bfloat16)


MESH = pl.DeviceIdType.MESH
PEERS = 3


def pick_tables():
    pick = np.zeros((160, 128), np.float32)
    back = np.zeros((128, 128), np.float32)
    for b in range(-2, 8):
        for a in range(16):
            t = 8 * a + b
            if t >= 0:
                pick[(b + 2) * 16 + a, t] = 1.0
                if b >= 0:
                    back[t, b * 16 + a] = 1.0
    return pick.astype(ml_dtypes.bfloat16), back.astype(ml_dtypes.bfloat16)


class Gather:
    def __init__(self, buf, per, sems, y, me):
        self.buf, self.per, self.sems, self.y, self.me = buf, per, sems, y, me

    def part(self, owner):
        return self.buf.at[pl.ds((owner * 2 + lax.rem(self.me, 2)) * self.per, self.per)]

    def across(self, r):
        mine = self.part(self.y)
        return pltpu.make_async_remote_copy(
            src_ref=mine, dst_ref=mine, send_sem=self.sems.at[0, r - 1], recv_sem=self.sems.at[1, r - 1],
            device_id={"lang": lax.rem(self.y + r, 4)}, device_id_type=MESH,
        )

    def beside(self, r):
        theirs = self.part(lax.rem(self.y + 4 - r, 4))
        return pltpu.make_async_remote_copy(
            src_ref=theirs, dst_ref=theirs, send_sem=self.sems.at[2, r - 1], recv_sem=self.sems.at[3, r - 1],
            device_id={"seq": self.me + 1 - 2 * lax.rem(self.me, 2)}, device_id_type=MESH,
        )

    def start(self):
        for r in (2, 1, 3):
            self.across(r).start()

    def sent(self):
        for r in (2, 1, 3):
            self.across(r).wait_send()

    def forward(self):
        for r in (1, 3, 2):
            self.across(r).wait_recv()
            self.beside(r).start()

    def finish(self):
        for r in (1, 3, 2):
            self.beside(r).wait_recv()
        for r in (1, 3, 2):
            self.beside(r).wait_send()


def columns(d, width=LANES):
    return pl.ds(pl.multiple_of(d * width, width), width)


def tap_rows(sel_ref, rows, cols):
    return jnp.concatenate(
        [jnp.broadcast_to(sel_ref[s, pl.ds(rows[s], 1), cols], (8, LANES)) for s in range(2)], 0
    )


def short_block(pos_ref, taps, b, cols):
    total = None
    for j in range(3):
        term = pos_ref[pl.ds((b + 2 - j) * 16, 16), cols] * taps[j]
        total = term if total is None else total + term
    return total


def fused_kernel(
    lang_ref, skip_ref, pick_ref, unpick_ref, q_in, k_in, v_in, taps_in, down_in, up_in, filt_in, table_in,
    back_in, step_in, out_ref,
    qv, kv, vv, qp, kp, vp, traw, t32, tq32, taps_kv, taps_q, tsel, tqsel, down_all, up_all, down2, up2,
    halo32, halo_out, halo_in, send_x, recv_x, filt, table, back, step, high, low, p, h, tw, g, send_y, recv_y,
    qs, gate, prod, out, local_sem, halo_sem, kv_sem, tq_sem, down_sem, up_sem, x_send, x_recv, y_send, y_recv,
    out_sem,
):
    y = lax.axis_index("lang")
    me = lax.axis_index("seq")
    loads = [
        pltpu.make_async_copy(src, dst, local_sem.at[i])
        for i, (src, dst) in enumerate([
            (taps_in, traw), (k_in.at[0], kv), (v_in.at[0], vv), (q_in.at[0], qv),
            (down_in, down_all.at[pl.ds(4 * y, 4)]), (up_in, up_all.at[pl.ds(4 * y, 4)]),
            (filt_in, filt), (table_in, table), (back_in, back), (step_in, step),
        ])
    ]
    for load in loads:
        load.start()

    barrier = pltpu.get_barrier_semaphore()
    for r in range(1, 4):
        pl.semaphore_signal(barrier, inc=1, device_id={"lang": lax.rem(y + r, 4)}, device_id_type=MESH)

    @pl.loop(1, 32)
    def _(r):
        pl.semaphore_signal(barrier, inc=1, device_id={"seq": lax.rem(me + r, 32)}, device_id_type=MESH)

    kv_get = Gather(taps_kv, 2, kv_sem, y, me)
    tq_get = Gather(taps_q, 1, tq_sem, y, me)
    down_get = Gather(down_all, 2, down_sem, y, me)
    up_get = Gather(up_all, 2, up_sem, y, me)

    t32[...] = jnp.zeros_like(t32)
    tq32[...] = jnp.zeros_like(tq32)
    loads[0].wait()
    for l in range(4):
        for j in range(3):
            three = traw[l, j].astype(jnp.float32)
            t32[l, pl.ds(2 * j, 2), :] = three[1:3]
            tq32[l // 2, pl.ds((l % 2) * 4 + j, 1), :] = three[0:1]
    taps_kv[pl.ds(4 * y, 4)] = t32[...].astype(jnp.bfloat16)
    taps_q[pl.ds(2 * y, 2)] = tq32[...].astype(jnp.bfloat16)
    pl.semaphore_wait(barrier, 34)
    kv_get.start()

    halo32[...] = jnp.zeros_like(halo32)
    for s, (load, raw, pos) in enumerate([(loads[1], kv, kp), (loads[2], vv, vp), (loads[3], qv, qp)]):
        load.wait()

        @pl.loop(0, 8)
        def _(i, raw=raw, pos=pos):
            cols = columns(i, 512)
            pos[:, cols] = jnp.dot(pick_ref[...], raw[:, cols], preferred_element_type=jnp.float32)

        halo32[pl.ds(2 * s, 1), :] = pos[pl.ds(143, 1), :]
        halo32[pl.ds(2 * s + 1, 1), :] = pos[pl.ds(159, 1), :]
    halo_out[...] = halo32[...].astype(jnp.bfloat16)
    halo = pltpu.make_async_remote_copy(
        src_ref=halo_out, dst_ref=halo_in, send_sem=halo_sem.at[0], recv_sem=halo_sem.at[1],
        device_id={"seq": lax.rem(me + 1, 32)}, device_id_type=MESH,
    )
    halo.start()

    kv_get.forward()
    tq_get.start()
    loads[4].wait()
    loads[5].wait()
    down_get.start()
    up_get.start()
    halo.wait_recv()
    halo32[...] = jnp.where(me > 0, halo_in[...].astype(jnp.float32), 0.0)
    for s, pos in enumerate([kp, vp, qp]):
        pos[pl.ds(0, 1), :] = halo32[pl.ds(2 * s, 1), :]
        pos[pl.ds(16, 1), :] = halo32[pl.ds(2 * s + 1, 1), :]
    kv_get.finish()
    langs = [lang_ref[0, s] for s in range(2)]
    for s in range(2):
        tsel[s] = taps_kv[langs[s]].astype(jnp.float32)

    def carrier(d, put):
        cols = columns(d)
        taps = [[tap_rows(tsel, (2 * j + n,) * 2, cols) for j in range(3)] for n in range(2)]
        for b in range(8):
            put(b, (short_block(kp, taps[0], b, cols) * short_block(vp, taps[1], b, cols)).astype(jnp.bfloat16))

    def x_copy(r):
        return pltpu.make_async_remote_copy(
            src_ref=send_x.at[r], dst_ref=recv_x.at[pl.ds(pl.multiple_of(me * 16, 16), 16), :],
            send_sem=x_send.at[r], recv_sem=x_recv.at[r],
            device_id={"seq": lax.bitwise_xor(me, r)}, device_id_type=MESH,
        )

    @pl.loop(1, 32)
    def _(r):
        def put(b, value):
            send_x[r, :, lane(b)] = value

        carrier(lax.bitwise_xor(me, r), put)
        x_copy(r).start()

    own = pl.ds(pl.multiple_of(me * 16, 16), 16)

    def put_own(b, value):
        recv_x[own, lane(b)] = value

    carrier(me, put_own)

    for load in loads[6:]:
        load.wait()
    filter_spectrum(filt, table, step, high, low, p, h, tw)

    @pl.loop(1, 32)
    def _(r):
        x_copy(r).wait_recv()

    stage_matmul(p, table, [recv_x])
    spectrum_product(p, h, tw, g)
    skip = skip_ref[pl.ds(me, 1), :]

    def y_copy(r):
        d = lax.bitwise_xor(me, r)
        return pltpu.make_async_remote_copy(
            src_ref=send_y.at[pl.ds(pl.multiple_of(d * 16, 16), 16), :], dst_ref=recv_y.at[me],
            send_sem=y_send.at[r], recv_sem=y_recv.at[r],
            device_id={"seq": d}, device_id_type=MESH,
        )

    for half in range(2):
        first = lax.bitwise_xor(lax.div(me, 16), half) * 256
        rows = pl.ds(pl.multiple_of(first, 256), 256)

        @pl.loop(0, 4)
        def _(i):
            cols = columns(i, 256)
            conv = jnp.dot(back[rows, :], g[:, cols], preferred_element_type=jnp.float32)
            both = jnp.concatenate([skip, skip], 1)
            send_y[rows, cols] = (conv + both * recv_x[rows, cols].astype(jnp.float32)).astype(jnp.bfloat16)

        @pl.loop(max(1, 16 * half), 16 * half + 16)
        def _(r):
            y_copy(r).start()

    tq_get.forward()
    down_get.forward()
    up_get.forward()
    tq_get.finish()
    for s in range(2):
        pair = taps_q[lax.div(langs[s], 2)].astype(jnp.float32)
        tqsel[s, 0:4, :] = jnp.where(lax.rem(langs[s], 2) > 0, pair[4:8], pair[0:4])

    @pl.loop(0, 32)
    def _(d):
        cols = columns(d)
        taps = [tap_rows(tqsel, (j, j), cols) for j in range(3)]
        for b in range(8):
            qs[pl.ds(b * 16, 16), cols] = short_block(qp, taps, b, cols).astype(jnp.bfloat16)

    down_get.finish()
    up_get.finish()
    for s in range(2):
        down2[pl.ds(16 * s, 16), :] = down_all[langs[s]]
        up2[pl.ds(16 * s, 16), :] = up_all[langs[s]]
    lows = lax.dot_general(
        qs[...], down2[...], (((1,), (1,)), ((), ())), preferred_element_type=jnp.float32
    )
    row_seg = lax.rem(lax.div(lax.broadcasted_iota(jnp.int32, (128, 32), 0), 8), 2)
    col_seg = lax.div(lax.broadcasted_iota(jnp.int32, (128, 32), 1), 16)
    lows = jnp.where(row_seg == col_seg, lows, 0.0).astype(jnp.bfloat16)

    @pl.loop(0, 8)
    def _(i):
        cols = columns(i, 512)
        gate[:, cols] = qs[:, cols].astype(jnp.float32) + jnp.dot(
            lows, up2[:, cols], preferred_element_type=jnp.float32
        )

    recv_y[me] = send_y[own, :]

    def out_copy(i):
        cols = columns(i, 256)
        return pltpu.make_async_copy(out.at[:, cols], out_ref.at[0, :, cols], out_sem.at[i])

    @pl.loop(0, 16)
    def _(i):
        chip = lax.bitwise_xor(lax.div(me, 2), i)
        cols = columns(chip, 256)

        @pl.when(i > 0)
        def _():
            y_copy(2 * i).wait_recv()

        y_copy(2 * i + 1).wait_recv()
        for core in range(2):
            s = 2 * chip + core
            for b in range(8):
                piece = gate[pl.ds(b * 16, 16), columns(s)] * recv_y[s, :, lane(b)].astype(jnp.float32)
                prod[pl.ds(b * 16, 16), lane(core)] = piece.astype(jnp.bfloat16)
        out[:, cols] = jnp.dot(
            unpick_ref[...], prod[...], preferred_element_type=jnp.float32
        ).astype(jnp.bfloat16)
        out_copy(chip).start()

    halo.wait_send()
    for get in (kv_get, tq_get, down_get, up_get):
        get.sent()

    @pl.loop(1, 32)
    def _(r):
        x_copy(r).wait_send()
        y_copy(r).wait_send()

    @pl.loop(0, 16)
    def _(i):
        out_copy(i).wait()


def local(q_stream, k_stream, v_stream, lang_ids, short_taps, adapter_down, adapter_up, long_filter, bypass_coefficient):
    fwd, back, step = dft_tables()
    pick, unpick = pick_tables()
    bf16, f32 = jnp.bfloat16, jnp.float32
    vmem = pl.BlockSpec(memory_space=pltpu.VMEM)
    anywhere = pl.BlockSpec(memory_space=pl.ANY)
    dma = pltpu.SemaphoreType.DMA
    arrays = [
        ((128, 4096), bf16), ((128, 4096), bf16), ((128, 4096), bf16),
        ((160, 4096), f32), ((160, 4096), f32), ((160, 4096), f32),
        ((4, 3, 3, 4096), bf16), ((4, 8, 4096), f32), ((2, 8, 4096), f32),
        ((16, 8, 4096), bf16), ((8, 8, 4096), bf16), ((2, 8, 4096), f32), ((2, 8, 4096), f32),
        ((16, 16, 4096), bf16), ((16, 16, 4096), bf16), ((32, 4096), bf16), ((32, 4096), bf16),
        ((8, 4096), f32), ((8, 4096), bf16), ((8, 4096), bf16),
        ((32, 16, 1024), bf16), ((512, 1024), bf16),
        ((4096, 128), f32), ((1024, 512), bf16), ((512, 1024), bf16), ((2, 512, 128), f32),
        ((512, 1024), bf16), ((512, 1024), bf16),
        ((1024, 1024), f32), ((1024, 1024), f32), ((1024, 1024), f32), ((1024, 1024), bf16),
        ((512, 1024), bf16), ((32, 16, 1024), bf16),
        ((128, 4096), bf16), ((128, 4096), f32), ((128, 256), bf16), ((128, 4096), bf16),
    ]
    return pl.pallas_call(
        fused_kernel,
        out_shape=jax.ShapeDtypeStruct(q_stream.shape, bf16),
        in_specs=[pl.BlockSpec(memory_space=pltpu.SMEM)] + [vmem] * 3 + [anywhere] * 10,
        out_specs=anywhere,
        scratch_shapes=[pltpu.VMEM(shape, kind) for shape, kind in arrays]
        + [dma((10,)), dma((2,)), dma((4, PEERS)), dma((4, PEERS)), dma((4, PEERS)), dma((4, PEERS))]
        + [dma((32,))] * 4
        + [dma((16,))],
        compiler_params=pltpu.CompilerParams(
            collective_id=0, has_side_effects=True, vmem_limit_bytes=60 << 20
        ),
    )(
        lang_ids, bypass_coefficient.reshape(32, 128), jnp.asarray(pick), jnp.asarray(unpick),
        q_stream, k_stream, v_stream, short_taps, adapter_down, adapter_up, long_filter,
        jnp.asarray(fwd), jnp.asarray(back), jnp.asarray(step),
    )


def solution(mesh):
    placed = (
        P("lang", "seq", None),
        P("lang", "seq", None),
        P("lang", "seq", None),
        P("lang", "seq"),
        P("lang", None, None, None),
        P("lang", None, None),
        P("lang", None, None),
        P(None, "seq"),
        P(),
    )
    return jax.shard_map(
        local, mesh=mesh, in_specs=placed, out_specs=P("lang", "seq", None), check_vma=False
    )
```

time: 133 us -> 67 us (0.50)
  Pallas kernels: 15.3 us -> 62.5 us
  waiting for transfers between devices: 28.5 us -> 0 us
  starting transfers between devices: 27.4 us -> 0 us
  local copies, waits for them, and re-layouts: 28.5 us -> 4.25 us
  other arithmetic: 14.8 us -> 0 us
  matrix products: 9.48 us -> 0 us
  blocking collectives: 7.32 us -> 0 us
    pallas_call x1, Pallas kernels: 15.3 us -> 62.5 us  [local(): pl.pallas_call(fused_kernel, out_shape=jax.ShapeDtypeStruct(q_stream.shap...]
    all_to_all x5 -> x0, waiting for transfers between devices: 28.5 us -> none  [the longest x1 9.5 us: local(): lax.all_to_all(modulating_cosine, 'seq', split_axis=1, concat_axis=0, til...]
    all_to_all x5 -> x0, starting transfers between devices: 22.5 us -> none  [the longest x1 8.02 us: local(): lax.all_to_all(modulating_cosine, 'seq', split_axis=1, concat_axis=0, til...]
    reshape x7 -> x0, local copies, waits for them, and re-layouts: 12.7 us -> none  [the longest x2 5.84 us: local(): send_up.reshape((groups, seg_count) + send_up.shape[1:])]
    dot_general x4 -> x0, matrix products: 9.48 us -> none  [the longest x1 5.99 us: local(): jnp.einsum('snr,srd->snd', low, up_mine, preferred_element_type=jnp.float32)]
    unnamed x1 -> x0, blocking collectives: 7.32 us -> none
    convert_element_type x4 -> x0, other arithmetic: 6.37 us -> none  [the longest x1 3.26 us: local(): modulating_cosine = (query_local_smoothed * payload_local_smoothed).astyp...]
    reduce_sum x3 -> x0, other arithmetic: 4.95 us -> none  [the longest x1 2.67 us: local(): up_mine = jnp.sum(got_up.astype(jnp.float32), axis=0).astype(jnp.bfloat16)]
  transfers between devices with their start and end apart: 6 -> 0, of which waited for: 4 -> 0; matrix products, arithmetic and copies ran while one was open for 29% -> 0% of each run, Pallas kernels for 12% -> 0%
where the time goes in v1:
time: 67 us; the launch traced here: 66.8 us
  Pallas kernels  62.5 us (93%)
  local copies, waits for them, and re-layouts  4.25 us (6%)
    pallas_call x1, Pallas kernels, local(): pl.pallas_call(fused_kernel, out_shape=jax.ShapeDtypeStruct(q_stream.shap...  62.5 us
    unnamed x2, local copies, waits for them, and re-layouts  4.25 us

profile of v1, /device:TPU:1, one launch (start us, length us, event | category | flops | bytes accessed | tf_op | source)
XLA Modules:
  0.0 66.8 jit_solution(5590970678382073424)
XLA Ops:
  0.0 2.0 %copy.15.taps_in = bf16[4,3,3,4096]{3,2,1,0:T(4,128)(2,1)} copy(bf16[4,3,3,4096]{3,0,2,1:T(4,128)(2,1)} %param.18) | data formatting | bytes 589824 | tf_op args[4]
  2.0 62.5 %shard_map.136 = bf16[1,128,4096]{2,1,0:T(8,128)(2,1)} custom-call(s32[1,2]{1,0:T(1,128)} %lang_ref.1, f32[32,128]{1,0:T(8,128)} %bitcast.1, bf16[160,128]{1,0:T(8,128)(2,1)} %constant.10.clone.pick_ref, bf16[128,128]{1,0:T(8,128)(2,1)} %constant.11.clone.unpick_ref, bf16[1,128,4096]{2,1,0:T(8,128)(2,1)} %q_in.1, bf16[1,128,4096]{2,1,0:T(8,128)(2,1)} %k_in.1, ...), custom_call_target="tpu_custom_call" | custom-call | tf_op jit(solution)/shard_map/pallas_call | solution.py:453
  64.5 2.3 %copy.17 = bf16[1,128,4096]{2,1,0:T(8,128)(2,1)} copy(bf16[1,128,4096]{2,1,0:T(8,128)(2,1)} %shard_map.136) | data formatting | bytes 2097152

commit v2 on v1

--- a/solution.py
+++ b/solution.py
@@ -136,7 +136,7 @@
 
 
 MESH = pl.DeviceIdType.MESH
-PEERS = 3
+GROUP = 2
 
 
 def pick_tables():
@@ -152,45 +152,25 @@
     return pick.astype(ml_dtypes.bfloat16), back.astype(ml_dtypes.bfloat16)
 
 
-class Gather:
-    def __init__(self, buf, per, sems, y, me):
-        self.buf, self.per, self.sems, self.y, self.me = buf, per, sems, y, me
-
-    def part(self, owner):
-        return self.buf.at[pl.ds((owner * 2 + lax.rem(self.me, 2)) * self.per, self.per)]
+class Panels:
+    def __init__(self, part, sems, y, me):
+        self.part, self.sems, self.y, self.me = part, sems, y, me
+
+    def move(self, owner, kind, r, device):
+        ref = self.part(owner)
+        return pltpu.make_async_remote_copy(
+            src_ref=ref, dst_ref=ref, send_sem=self.sems.at[kind, r - 1], recv_sem=self.sems.at[kind + 1, r - 1],
+            device_id=device, device_id_type=MESH,
+        )
 
     def across(self, r):
-        mine = self.part(self.y)
-        return pltpu.make_async_remote_copy(
-            src_ref=mine, dst_ref=mine, send_sem=self.sems.at[0, r - 1], recv_sem=self.sems.at[1, r - 1],
-            device_id={"lang": lax.rem(self.y + r, 4)}, device_id_type=MESH,
-        )
+        return self.move(self.y, 0, r, {"lang": lax.rem(self.y + r, 4)})
+
+    def relay(self, r):
+        return self.move(lax.rem(self.y + 4 - r, 4), 0, 2, {"lang": lax.rem(self.y + r, 4)})
 
     def beside(self, r):
-        theirs = self.part(lax.rem(self.y + 4 - r, 4))
-        return pltpu.make_async_remote_copy(
-            src_ref=theirs, dst_ref=theirs, send_sem=self.sems.at[2, r - 1], recv_sem=self.sems.at[3, r - 1],
-            device_id={"seq": self.me + 1 - 2 * lax.rem(self.me, 2)}, device_id_type=MESH,
-        )
-
-    def start(self):
-        for r in (2, 1, 3):
-            self.across(r).start()
-
-    def sent(self):
-        for r in (2, 1, 3):
-            self.across(r).wait_send()
-
-    def forward(self):
-        for r in (1, 3, 2):
-            self.across(r).wait_recv()
-            self.beside(r).start()
-
-    def finish(self):
-        for r in (1, 3, 2):
-            self.beside(r).wait_recv()
-        for r in (1, 3, 2):
-            self.beside(r).wait_send()
+        return self.move(lax.rem(self.y + 4 - r, 4), 2, r, {"seq": lax.bitwise_xor(self.me, 1)})
 
 
 def columns(d, width=LANES):
@@ -214,13 +194,15 @@
 def fused_kernel(
     lang_ref, skip_ref, pick_ref, unpick_ref, q_in, k_in, v_in, taps_in, down_in, up_in, filt_in, table_in,
     back_in, step_in, out_ref,
-    qv, kv, vv, qp, kp, vp, traw, t32, tq32, taps_kv, taps_q, tsel, tqsel, down_all, up_all, down2, up2,
+    qv, kv, vv, qp, kp, vp, traw, tk_0, tk_1, tk_2, tk_3, tq_all, tsel, tqsel, down_all, up_all, down2, up2,
     halo32, halo_out, halo_in, send_x, recv_x, filt, table, back, step, high, low, p, h, tw, g, send_y, recv_y,
-    qs, gate, prod, out, local_sem, halo_sem, kv_sem, tq_sem, down_sem, up_sem, x_send, x_recv, y_send, y_recv,
-    out_sem,
+    qs, gate, prod, out, local_sem, halo_sem, tk_sem, tq_sem, down_sem, up_sem, x_send, x_recv, y_send, y_recv,
+    out_sem, line_sem, all_sem,
 ):
     y = lax.axis_index("lang")
     me = lax.axis_index("seq")
+    core = lax.rem(me, 2)
+    tk_all = [tk_0, tk_1, tk_2, tk_3]
     loads = [
         pltpu.make_async_copy(src, dst, local_sem.at[i])
         for i, (src, dst) in enumerate([
@@ -235,28 +217,31 @@
     barrier = pltpu.get_barrier_semaphore()
     for r in range(1, 4):
         pl.semaphore_signal(barrier, inc=1, device_id={"lang": lax.rem(y + r, 4)}, device_id_type=MESH)
-
-    @pl.loop(1, 32)
-    def _(r):
-        pl.semaphore_signal(barrier, inc=1, device_id={"seq": lax.rem(me + r, 32)}, device_id_type=MESH)
-
-    kv_get = Gather(taps_kv, 2, kv_sem, y, me)
-    tq_get = Gather(taps_q, 1, tq_sem, y, me)
-    down_get = Gather(down_all, 2, down_sem, y, me)
-    up_get = Gather(up_all, 2, up_sem, y, me)
-
-    t32[...] = jnp.zeros_like(t32)
-    tq32[...] = jnp.zeros_like(tq32)
+    for r in (1, 2, 4, 6, 8, 16, 24):
+        pl.semaphore_signal(barrier, inc=1, device_id={"seq": lax.bitwise_xor(me, r)}, device_id_type=MESH)
+    pl.semaphore_signal(barrier, inc=1, device_id={"seq": lax.rem(me + 31, 32)}, device_id_type=MESH)
+
+    def chip_of(i, j):
+        return lax.bitwise_xor(lax.div(me, 2), 4 * j + lax.bitwise_xor(j, i))
+
+    half = pl.ds(pl.multiple_of(core * 512, 512), 512)
+    halves = pl.ds(pl.multiple_of(core * 2048, 2048), 2048)
+    chunks = [
+        Panels(lambda owner, i=i: tk_all[i].at[owner, :, :, half], tk_sem.at[i], y, me) for i in range(4)
+    ]
+    tq_get = Panels(lambda owner: tq_all.at[owner, :, :, halves], tq_sem, y, me)
+    down_get = Panels(lambda owner: down_all.at[pl.ds(4 * owner + 2 * core, 2)], down_sem, y, me)
+    up_get = Panels(lambda owner: up_all.at[pl.ds(4 * owner + 2 * core, 2)], up_sem, y, me)
+
     loads[0].wait()
-    for l in range(4):
-        for j in range(3):
-            three = traw[l, j].astype(jnp.float32)
-            t32[l, pl.ds(2 * j, 2), :] = three[1:3]
-            tq32[l // 2, pl.ds((l % 2) * 4 + j, 1), :] = three[0:1]
-    taps_kv[pl.ds(4 * y, 4)] = t32[...].astype(jnp.bfloat16)
-    taps_q[pl.ds(2 * y, 2)] = tq32[...].astype(jnp.bfloat16)
-    pl.semaphore_wait(barrier, 34)
-    kv_get.start()
+    for i in range(4):
+        for j in range(4):
+            cols = columns(chip_of(i, j), 256)
+            for t in range(3):
+                for n in range(2):
+                    tk_all[i][y, 2 * t + n, :, 256 * j:256 * j + 256] = traw[t, n + 1, :, cols]
+    for t in range(3):
+        tq_all[y, t] = traw[t, 0]
 
     halo32[...] = jnp.zeros_like(halo32)
     for s, (load, raw, pos) in enumerate([(loads[1], kv, kp), (loads[2], vv, vp), (loads[3], qv, qp)]):
@@ -270,31 +255,44 @@
         halo32[pl.ds(2 * s, 1), :] = pos[pl.ds(143, 1), :]
         halo32[pl.ds(2 * s + 1, 1), :] = pos[pl.ds(159, 1), :]
     halo_out[...] = halo32[...].astype(jnp.bfloat16)
+
+    pl.semaphore_wait(barrier, 11)
+    for get in chunks:
+        for r in (2, 1, 3):
+            get.across(r).start()
     halo = pltpu.make_async_remote_copy(
         src_ref=halo_out, dst_ref=halo_in, send_sem=halo_sem.at[0], recv_sem=halo_sem.at[1],
         device_id={"seq": lax.rem(me + 1, 32)}, device_id_type=MESH,
     )
     halo.start()
-
-    kv_get.forward()
-    tq_get.start()
-    loads[4].wait()
-    loads[5].wait()
-    down_get.start()
-    up_get.start()
+    for r in (2, 4, 6):
+        pl.semaphore_signal(line_sem, inc=1, device_id={"seq": lax.bitwise_xor(me, r)}, device_id_type=MESH)
+    pl.semaphore_wait(line_sem, 3)
+    pl.semaphore_signal(all_sem, inc=1, device_id={"seq": lax.bitwise_xor(me, 1)}, device_id_type=MESH)
+
+    def hand_on(get):
+        for r in (1, 3, 2):
+            get.across(r).wait_recv()
+            get.beside(r).start()
+
+    hand_on(chunks[0])
     halo.wait_recv()
     halo32[...] = jnp.where(me > 0, halo_in[...].astype(jnp.float32), 0.0)
     for s, pos in enumerate([kp, vp, qp]):
         pos[pl.ds(0, 1), :] = halo32[pl.ds(2 * s, 1), :]
         pos[pl.ds(16, 1), :] = halo32[pl.ds(2 * s + 1, 1), :]
-    kv_get.finish()
-    langs = [lang_ref[0, s] for s in range(2)]
-    for s in range(2):
-        tsel[s] = taps_kv[langs[s]].astype(jnp.float32)
-
-    def carrier(d, put):
+    pl.semaphore_wait(all_sem, 1)
+
+    owners = [lax.div(lang_ref[0, s], 4) for s in range(2)]
+    places = [lax.rem(lang_ref[0, s], 4) for s in range(2)]
+
+    def chosen(four, s):
+        row = lax.broadcasted_iota(jnp.int32, four.shape, 0)
+        return jnp.sum(jnp.where(row == places[s], four.astype(jnp.float32), 0.0), axis=0, keepdims=True)
+
+    def carrier(d, tap_cols, put):
         cols = columns(d)
-        taps = [[tap_rows(tsel, (2 * j + n,) * 2, cols) for j in range(3)] for n in range(2)]
+        taps = [[tap_rows(tsel, (2 * j + n,) * 2, tap_cols) for j in range(3)] for n in range(2)]
         for b in range(8):
             put(b, (short_block(kp, taps[0], b, cols) * short_block(vp, taps[1], b, cols)).astype(jnp.bfloat16))
 
@@ -305,24 +303,48 @@
             device_id={"seq": lax.bitwise_xor(me, r)}, device_id_type=MESH,
         )
 
-    @pl.loop(1, 32)
-    def _(r):
-        def put(b, value):
-            send_x[r, :, lane(b)] = value
-
-        carrier(lax.bitwise_xor(me, r), put)
-        x_copy(r).start()
-
+    for i in range(4):
+        for r in (1, 3, 2):
+            chunks[i].beside(r).wait_recv()
+        if i < 3:
+            hand_on(chunks[i + 1])
+        for s in range(2):
+            for n in range(6):
+                tsel[s, pl.ds(n, 1), 1024 * i:1024 * i + 1024] = chosen(tk_all[i][owners[s], n], s)
+
+        @pl.loop(1 if i == 0 else 0, 8)
+        def _(k, i=i):
+            j, flip = lax.div(k, 2), lax.rem(k, 2)
+            r = 8 * j + 2 * lax.bitwise_xor(j, i) + flip
+
+            def put(b, value):
+                send_x[r, :, lane(b)] = value
+
+            carrier(lax.bitwise_xor(me, r), columns(8 * i + 2 * j + lax.bitwise_xor(core, flip)), put)
+            x_copy(r).start()
+
+        if i == 2:
+            loads[4].wait()
+            for get in (tq_get, down_get):
+                for r in (2, 1, 3) if get is tq_get else (1, 3):
+                    get.across(r).start()
+
+    loads[5].wait()
+    for r in (3, 1):
+        up_get.across(r).start()
     own = pl.ds(pl.multiple_of(me * 16, 16), 16)
 
     def put_own(b, value):
         recv_x[own, lane(b)] = value
 
-    carrier(me, put_own)
+    carrier(me, columns(core), put_own)
 
     for load in loads[6:]:
         load.wait()
     filter_spectrum(filt, table, step, high, low, p, h, tw)
+    down_get.across(1).wait_recv()
+    down_get.relay(1).start()
+    down_get.beside(1).start()
 
     @pl.loop(1, 32)
     def _(r):
@@ -334,34 +356,49 @@
 
     def y_copy(r):
         d = lax.bitwise_xor(me, r)
+        j = lax.div(r, 8)
+        i = lax.bitwise_xor(lax.rem(lax.div(r, 2), 4), j)
+        slot = 8 * i + 2 * j + lax.rem(d, 2)
         return pltpu.make_async_remote_copy(
-            src_ref=send_y.at[pl.ds(pl.multiple_of(d * 16, 16), 16), :], dst_ref=recv_y.at[me],
+            src_ref=send_y.at[pl.ds(pl.multiple_of(slot * 16, 16), 16), :], dst_ref=recv_y.at[me],
             send_sem=y_send.at[r], recv_sem=y_recv.at[r],
             device_id={"seq": d}, device_id_type=MESH,
         )
 
-    for half in range(2):
-        first = lax.bitwise_xor(lax.div(me, 16), half) * 256
-        rows = pl.ds(pl.multiple_of(first, 256), 256)
+    for i in range(0, 4, GROUP):
+        blocks = [
+            pl.ds(pl.multiple_of(32 * chip_of(i + n, j), 32), 32) for n in range(GROUP) for j in range(4)
+        ]
 
         @pl.loop(0, 4)
-        def _(i):
-            cols = columns(i, 256)
-            conv = jnp.dot(back[rows, :], g[:, cols], preferred_element_type=jnp.float32)
+        def _(m, i=i, blocks=blocks):
+            cols = columns(m, 256)
+            left = jnp.concatenate([back[rows, :] for rows in blocks], 0)
+            signal = jnp.concatenate([recv_x[rows, cols] for rows in blocks], 0)
+            conv = jnp.dot(left, g[:, cols], preferred_element_type=jnp.float32)
             both = jnp.concatenate([skip, skip], 1)
-            send_y[rows, cols] = (conv + both * recv_x[rows, cols].astype(jnp.float32)).astype(jnp.bfloat16)
-
-        @pl.loop(max(1, 16 * half), 16 * half + 16)
-        def _(r):
-            y_copy(r).start()
-
-    tq_get.forward()
-    down_get.forward()
-    up_get.forward()
-    tq_get.finish()
+            send_y[128 * i:128 * (i + GROUP), cols] = (conv + both * signal.astype(jnp.float32)).astype(jnp.bfloat16)
+
+        @pl.loop(8 * i + (1 if i == 0 else 0), 8 * (i + GROUP))
+        def _(k):
+            n, j, flip = lax.div(k, 8), lax.rem(lax.div(k, 2), 4), lax.rem(k, 2)
+            y_copy(8 * j + 2 * lax.bitwise_xor(j, n) + flip).start()
+
+    up_get.across(3).wait_recv()
+    up_get.relay(3).start()
+    up_get.beside(3).start()
+    for r in (1, 3, 2):
+        tq_get.across(r).wait_recv()
+        tq_get.beside(r).start()
+    down_get.across(3).wait_recv()
+    down_get.beside(3).start()
+    up_get.across(1).wait_recv()
+    up_get.beside(1).start()
+    for r in (1, 3, 2):
+        tq_get.beside(r).wait_recv()
     for s in range(2):
-        pair = taps_q[lax.div(langs[s], 2)].astype(jnp.float32)
-        tqsel[s, 0:4, :] = jnp.where(lax.rem(langs[s], 2) > 0, pair[4:8], pair[0:4])
+        for t in range(3):
+            tqsel[s, pl.ds(t, 1), :] = chosen(tq_all[owners[s], t], s)
 
     @pl.loop(0, 32)
     def _(d):
@@ -370,11 +407,15 @@
         for b in range(8):
             qs[pl.ds(b * 16, 16), cols] = short_block(qp, taps, b, cols).astype(jnp.bfloat16)
 
-    down_get.finish()
-    up_get.finish()
+    for get in (down_get, up_get):
+        get.across(2).wait_recv()
+        get.beside(2).start()
+    for get in (down_get, up_get):
+        for r in (1, 3, 2):
+            get.beside(r).wait_recv()
     for s in range(2):
-        down2[pl.ds(16 * s, 16), :] = down_all[langs[s]]
-        up2[pl.ds(16 * s, 16), :] = up_all[langs[s]]
+        down2[pl.ds(16 * s, 16), :] = down_all[lang_ref[0, s]]
+        up2[pl.ds(16 * s, 16), :] = up_all[lang_ref[0, s]]
     lows = lax.dot_general(
         qs[...], down2[...], (((1,), (1,)), ((), ())), preferred_element_type=jnp.float32
     )
@@ -389,35 +430,45 @@
             lows, up2[:, cols], preferred_element_type=jnp.float32
         )
 
-    recv_y[me] = send_y[own, :]
+    recv_y[me] = send_y[pl.ds(pl.multiple_of(core * 16, 16), 16), :]
 
     def out_copy(i):
         cols = columns(i, 256)
         return pltpu.make_async_copy(out.at[:, cols], out_ref.at[0, :, cols], out_sem.at[i])
 
     @pl.loop(0, 16)
-    def _(i):
-        chip = lax.bitwise_xor(lax.div(me, 2), i)
+    def _(k):
+        n, j = lax.div(k, 4), lax.rem(k, 4)
+        r = 8 * j + 2 * lax.bitwise_xor(j, n)
+        chip = lax.bitwise_xor(lax.div(me, 2), lax.div(r, 2))
         cols = columns(chip, 256)
 
-        @pl.when(i > 0)
+        @pl.when(k > 0)
         def _():
-            y_copy(2 * i).wait_recv()
-
-        y_copy(2 * i + 1).wait_recv()
-        for core in range(2):
-            s = 2 * chip + core
+            y_copy(r).wait_recv()
+
+        y_copy(r + 1).wait_recv()
+        for one in range(2):
+            s = 2 * chip + one
             for b in range(8):
                 piece = gate[pl.ds(b * 16, 16), columns(s)] * recv_y[s, :, lane(b)].astype(jnp.float32)
-                prod[pl.ds(b * 16, 16), lane(core)] = piece.astype(jnp.bfloat16)
+                prod[pl.ds(b * 16, 16), lane(one)] = piece.astype(jnp.bfloat16)
         out[:, cols] = jnp.dot(
             unpick_ref[...], prod[...], preferred_element_type=jnp.float32
         ).astype(jnp.bfloat16)
         out_copy(chip).start()
 
     halo.wait_send()
-    for get in (kv_get, tq_get, down_get, up_get):
-        get.sent()
+    for get in chunks + [tq_get]:
+        for r in (1, 2, 3):
+            get.across(r).wait_send()
+            get.beside(r).wait_send()
+    for get, way in ((down_get, 1), (up_get, 3)):
+        for r in (1, 3):
+            get.across(r).wait_send()
+        get.relay(way).wait_send()
+        for r in (1, 2, 3):
+            get.beside(r).wait_send()
 
     @pl.loop(1, 32)
     def _(r):
@@ -439,8 +490,8 @@
     arrays = [
         ((128, 4096), bf16), ((128, 4096), bf16), ((128, 4096), bf16),
         ((160, 4096), f32), ((160, 4096), f32), ((160, 4096), f32),
-        ((4, 3, 3, 4096), bf16), ((4, 8, 4096), f32), ((2, 8, 4096), f32),
-        ((16, 8, 4096), bf16), ((8, 8, 4096), bf16), ((2, 8, 4096), f32), ((2, 8, 4096), f32),
+        ((3, 3, 4, 4096), bf16), ] + [((4, 6, 4, 1024), bf16)] * 4 + [((4, 3, 4, 4096), bf16),
+        ((2, 8, 4096), f32), ((2, 8, 4096), f32),
         ((16, 16, 4096), bf16), ((16, 16, 4096), bf16), ((32, 4096), bf16), ((32, 4096), bf16),
         ((8, 4096), f32), ((8, 4096), bf16), ((8, 4096), bf16),
         ((32, 16, 1024), bf16), ((512, 1024), bf16),
@@ -456,15 +507,15 @@
         in_specs=[pl.BlockSpec(memory_space=pltpu.SMEM)] + [vmem] * 3 + [anywhere] * 10,
         out_specs=anywhere,
         scratch_shapes=[pltpu.VMEM(shape, kind) for shape, kind in arrays]
-        + [dma((10,)), dma((2,)), dma((4, PEERS)), dma((4, PEERS)), dma((4, PEERS)), dma((4, PEERS))]
+        + [dma((10,)), dma((2,)), dma((4, 4, 3)), dma((4, 3)), dma((4, 3)), dma((4, 3))]
         + [dma((32,))] * 4
-        + [dma((16,))],
+        + [dma((16,)), pltpu.SemaphoreType.REGULAR, pltpu.SemaphoreType.REGULAR],
         compiler_params=pltpu.CompilerParams(
             collective_id=0, has_side_effects=True, vmem_limit_bytes=60 << 20
         ),
     )(
         lang_ids, bypass_coefficient.reshape(32, 128), jnp.asarray(pick), jnp.asarray(unpick),
-        q_stream, k_stream, v_stream, short_taps, adapter_down, adapter_up, long_filter,
+        q_stream, k_stream, v_stream, short_taps.transpose(1, 2, 0, 3), adapter_down, adapter_up, long_filter,
         jnp.asarray(fwd), jnp.asarray(back), jnp.asarray(step),
     )
 

time: 67 us -> 60.2 us (0.90)
  Pallas kernels: 62.5 us -> 57.7 us
  local copies, waits for them, and re-layouts: 4.25 us -> 2.29 us
    pallas_call x1, Pallas kernels: 62.5 us -> 57.7 us  [local(): pl.pallas_call(fused_kernel, out_shape=jax.ShapeDtypeStruct(q_stream.shap...]
    unnamed x2 -> x1, local copies, waits for them, and re-layouts: 4.25 us -> 2.29 us
where the time goes in v2:
time: 60.2 us; the launch traced here: 60 us
  Pallas kernels  57.7 us (96%)
  local copies, waits for them, and re-layouts  2.29 us (4%)
    pallas_call x1, Pallas kernels, local(): pl.pallas_call(fused_kernel, out_shape=jax.ShapeDtypeStruct(q_stream.shap...  57.7 us
    unnamed x1, local copies, waits for them, and re-layouts  2.29 us

profile of v2, /device:TPU:1, one launch (start us, length us, event | category | flops | bytes accessed | tf_op | source)
XLA Modules:
  0.0 60.0 jit_solution(17637272678473256466)
XLA Ops:
  0.0 57.7 %shard_map.136 = bf16[1,128,4096]{2,1,0:T(8,128)(2,1)} custom-call(s32[1,2]{1,0:T(1,128)} %lang_ref.1, f32[32,128]{1,0:T(8,128)} %bitcast.3, bf16[160,128]{1,0:T(8,128)(2,1)} %constant.10.clone.pick_ref, bf16[128,128]{1,0:T(8,128)(2,1)} %constant.11.clone.unpick_ref, bf16[1,128,4096]{2,1,0:T(8,128)(2,1)} %q_in.1, bf16[1,128,4096]{2,1,0:T(8,128)(2,1)} %k_in.1, ...), custom_call_target="tpu_custom_call" | custom-call | tf_op jit(solution)/shard_map/pallas_call | solution.py:504
  57.7 2.3 %copy.16 = bf16[1,128,4096]{2,1,0:T(8,128)(2,1)} copy(bf16[1,128,4096]{2,1,0:T(8,128)(2,1)} %shard_map.136) | data formatting | bytes 2097152

commit v3 on v2

--- a/solution.py
+++ b/solution.py
@@ -224,10 +224,9 @@
     def chip_of(i, j):
         return lax.bitwise_xor(lax.div(me, 2), 4 * j + lax.bitwise_xor(j, i))
 
-    half = pl.ds(pl.multiple_of(core * 512, 512), 512)
     halves = pl.ds(pl.multiple_of(core * 2048, 2048), 2048)
     chunks = [
-        Panels(lambda owner, i=i: tk_all[i].at[owner, :, :, half], tk_sem.at[i], y, me) for i in range(4)
+        Panels(lambda owner, i=i: tk_all[i].at[owner], tk_sem.at[i], y, me) for i in range(4)
     ]
     tq_get = Panels(lambda owner: tq_all.at[owner, :, :, halves], tq_sem, y, me)
     down_get = Panels(lambda owner: down_all.at[pl.ds(4 * owner + 2 * core, 2)], down_sem, y, me)
@@ -244,45 +243,43 @@
         tq_all[y, t] = traw[t, 0]
 
     halo32[...] = jnp.zeros_like(halo32)
-    for s, (load, raw, pos) in enumerate([(loads[1], kv, kp), (loads[2], vv, vp), (loads[3], qv, qp)]):
+    for s, (load, raw) in enumerate([(loads[1], kv), (loads[2], vv), (loads[3], qv)]):
         load.wait()
-
-        @pl.loop(0, 8)
-        def _(i, raw=raw, pos=pos):
-            cols = columns(i, 512)
-            pos[:, cols] = jnp.dot(pick_ref[...], raw[:, cols], preferred_element_type=jnp.float32)
-
-        halo32[pl.ds(2 * s, 1), :] = pos[pl.ds(143, 1), :]
-        halo32[pl.ds(2 * s + 1, 1), :] = pos[pl.ds(159, 1), :]
+        halo32[pl.ds(2 * s, 2), :] = raw[112:128, :].astype(jnp.float32)[14:16]
     halo_out[...] = halo32[...].astype(jnp.bfloat16)
 
     pl.semaphore_wait(barrier, 11)
-    for get in chunks:
-        for r in (2, 1, 3):
-            get.across(r).start()
     halo = pltpu.make_async_remote_copy(
         src_ref=halo_out, dst_ref=halo_in, send_sem=halo_sem.at[0], recv_sem=halo_sem.at[1],
         device_id={"seq": lax.rem(me + 1, 32)}, device_id_type=MESH,
     )
-    halo.start()
+    for i, get in enumerate(chunks):
+        for r in (2, 1, 3):
+            get.across(r).start()
+        if i == 0:
+            halo.start()
     for r in (2, 4, 6):
         pl.semaphore_signal(line_sem, inc=1, device_id={"seq": lax.bitwise_xor(me, r)}, device_id_type=MESH)
     pl.semaphore_wait(line_sem, 3)
     pl.semaphore_signal(all_sem, inc=1, device_id={"seq": lax.bitwise_xor(me, 1)}, device_id_type=MESH)
 
-    def hand_on(get):
-        for r in (1, 3, 2):
-            get.across(r).wait_recv()
-            get.beside(r).start()
-
-    hand_on(chunks[0])
+    def picked(raw, pos):
+        @pl.loop(0, 8)
+        def _(i):
+            cols = columns(i, 512)
+            pos[:, cols] = jnp.dot(pick_ref[...], raw[:, cols], preferred_element_type=jnp.float32)
+
+    def rimmed(s, pos):
+        pos[pl.ds(0, 1), :] = halo32[pl.ds(2 * s, 1), :]
+        pos[pl.ds(16, 1), :] = halo32[pl.ds(2 * s + 1, 1), :]
+
+    picked(kv, kp)
+    picked(vv, vp)
     halo.wait_recv()
     halo32[...] = jnp.where(me > 0, halo_in[...].astype(jnp.float32), 0.0)
-    for s, pos in enumerate([kp, vp, qp]):
-        pos[pl.ds(0, 1), :] = halo32[pl.ds(2 * s, 1), :]
-        pos[pl.ds(16, 1), :] = halo32[pl.ds(2 * s + 1, 1), :]
+    rimmed(0, kp)
+    rimmed(1, vp)
     pl.semaphore_wait(all_sem, 1)
-
     owners = [lax.div(lang_ref[0, s], 4) for s in range(2)]
     places = [lax.rem(lang_ref[0, s], 4) for s in range(2)]
 
@@ -305,9 +302,7 @@
 
     for i in range(4):
         for r in (1, 3, 2):
-            chunks[i].beside(r).wait_recv()
-        if i < 3:
-            hand_on(chunks[i + 1])
+            chunks[i].across(r).wait_recv()
         for s in range(2):
             for n in range(6):
                 tsel[s, pl.ds(n, 1), 1024 * i:1024 * i + 1024] = chosen(tk_all[i][owners[s], n], s)
@@ -338,6 +333,8 @@
         recv_x[own, lane(b)] = value
 
     carrier(me, columns(core), put_own)
+    picked(qv, qp)
+    rimmed(2, qp)
 
     for load in loads[6:]:
         load.wait()
@@ -462,7 +459,8 @@
     for get in chunks + [tq_get]:
         for r in (1, 2, 3):
             get.across(r).wait_send()
-            get.beside(r).wait_send()
+    for r in (1, 2, 3):
+        tq_get.beside(r).wait_send()
     for get, way in ((down_get, 1), (up_get, 3)):
         for r in (1, 3):
             get.across(r).wait_send()

time: 60.2 us -> 54.4 us (0.904)
  Pallas kernels: 57.7 us -> 51.9 us
    pallas_call x1, Pallas kernels: 57.7 us -> 51.9 us  [local(): pl.pallas_call(fused_kernel, out_shape=jax.ShapeDtypeStruct(q_stream.shap...]
where the time goes in v3:
time: 54.4 us; the launch traced here: 54.2 us
  Pallas kernels  51.9 us (95%)
  local copies, waits for them, and re-layouts  2.29 us (4%)
    pallas_call x1, Pallas kernels, local(): pl.pallas_call(fused_kernel, out_shape=jax.ShapeDtypeStruct(q_stream.shap...  51.9 us
    unnamed x1, local copies, waits for them, and re-layouts  2.29 us

profile of v3, /device:TPU:1, one launch (start us, length us, event | category | flops | bytes accessed | tf_op | source)
XLA Modules:
  0.0 54.2 jit_solution(15643279142921887116)
XLA Ops:
  0.0 51.9 %shard_map.136 = bf16[1,128,4096]{2,1,0:T(8,128)(2,1)} custom-call(s32[1,2]{1,0:T(1,128)} %lang_ref.1, f32[32,128]{1,0:T(8,128)} %bitcast.3, bf16[160,128]{1,0:T(8,128)(2,1)} %constant.10.clone.pick_ref, bf16[128,128]{1,0:T(8,128)(2,1)} %constant.11.clone.unpick_ref, bf16[1,128,4096]{2,1,0:T(8,128)(2,1)} %q_in.1, bf16[1,128,4096]{2,1,0:T(8,128)(2,1)} %k_in.1, ...), custom_call_target="tpu_custom_call" | custom-call | tf_op jit(solution)/shard_map/pallas_call | solution.py:502
  51.9 2.3 %copy.16 = bf16[1,128,4096]{2,1,0:T(8,128)(2,1)} copy(bf16[1,128,4096]{2,1,0:T(8,128)(2,1)} %shard_map.136) | data formatting | bytes 2097152

commit v4 on v3

--- a/solution.py
+++ b/solution.py
@@ -10,7 +10,7 @@
 from jax.sharding import PartitionSpec as P
 
 LANES = 128
-ROWS = 16
+ROWS = 32
 
 
 def dft_tables():
@@ -70,7 +70,7 @@
     return slice(b * LANES, (b + 1) * LANES)
 
 
-def stage_matmul(out_ref, left_ref, right_refs, width=256):
+def stage_matmul(out_ref, left_ref, right_refs, width=512):
     columns = out_ref.shape[1]
 
     @pl.loop(0, columns // width)
@@ -196,7 +196,7 @@
     back_in, step_in, out_ref,
     qv, kv, vv, qp, kp, vp, traw, tk_0, tk_1, tk_2, tk_3, tq_all, tsel, tqsel, down_all, up_all, down2, up2,
     halo32, halo_out, halo_in, send_x, recv_x, filt, table, back, step, high, low, p, h, tw, g, send_y, recv_y,
-    qs, gate, prod, out, local_sem, halo_sem, tk_sem, tq_sem, down_sem, up_sem, x_send, x_recv, y_send, y_recv,
+    qs, gate, prod, out, back_sent, local_sem, halo_sem, tk_sem, tq_sem, down_sem, up_sem, x_send, x_recv, y_send, y_recv,
     out_sem, line_sem, all_sem,
 ):
     y = lax.axis_index("lang")
@@ -339,6 +339,10 @@
     for load in loads[6:]:
         load.wait()
     filter_spectrum(filt, table, step, high, low, p, h, tw)
+    for n in range(16):
+        rows = pl.ds(pl.multiple_of(32 * chip_of(n // 4, n % 4), 32), 32)
+        back_sent[32 * n:32 * n + 32, :] = back[rows, :]
+
     down_get.across(1).wait_recv()
     down_get.relay(1).start()
     down_get.beside(1).start()
@@ -363,18 +367,18 @@
         )
 
     for i in range(0, 4, GROUP):
-        blocks = [
-            pl.ds(pl.multiple_of(32 * chip_of(i + n, j), 32), 32) for n in range(GROUP) for j in range(4)
-        ]
-
-        @pl.loop(0, 4)
-        def _(m, i=i, blocks=blocks):
-            cols = columns(m, 256)
-            left = jnp.concatenate([back[rows, :] for rows in blocks], 0)
-            signal = jnp.concatenate([recv_x[rows, cols] for rows in blocks], 0)
-            conv = jnp.dot(left, g[:, cols], preferred_element_type=jnp.float32)
-            both = jnp.concatenate([skip, skip], 1)
-            send_y[128 * i:128 * (i + GROUP), cols] = (conv + both * signal.astype(jnp.float32)).astype(jnp.bfloat16)
+        @pl.loop(0, 2)
+        def _(m, i=i):
+            cols = columns(m, 512)
+            both = jnp.concatenate([skip] * 4, 1)
+            conv = jnp.dot(
+                back_sent[128 * i:128 * (i + GROUP), :], g[:, cols], preferred_element_type=jnp.float32
+            )
+            for n in range(4 * GROUP):
+                rows = pl.ds(pl.multiple_of(32 * chip_of(i + n // 4, n % 4), 32), 32)
+                send_y[128 * i + 32 * n:128 * i + 32 * n + 32, cols] = (
+                    conv[32 * n:32 * n + 32] + both * recv_x[rows, cols].astype(jnp.float32)
+                ).astype(jnp.bfloat16)
 
         @pl.loop(8 * i + (1 if i == 0 else 0), 8 * (i + GROUP))
         def _(k):
@@ -497,7 +501,7 @@
         ((512, 1024), bf16), ((512, 1024), bf16),
         ((1024, 1024), f32), ((1024, 1024), f32), ((1024, 1024), f32), ((1024, 1024), bf16),
         ((512, 1024), bf16), ((32, 16, 1024), bf16),
-        ((128, 4096), bf16), ((128, 4096), f32), ((128, 256), bf16), ((128, 4096), bf16),
+        ((128, 4096), bf16), ((128, 4096), f32), ((128, 256), bf16), ((128, 4096), bf16), ((512, 1024), bf16),
     ]
     return pl.pallas_call(
         fused_kernel,

time: 54.4 us -> 53.4 us (0.982)
  Pallas kernels: 51.9 us -> 50.9 us
    pallas_call x1, Pallas kernels: 51.9 us -> 50.9 us  [local(): pl.pallas_call(fused_kernel, out_shape=jax.ShapeDtypeStruct(q_stream.shap...]
where the time goes in v4:
time: 53.4 us; the launch traced here: 53.2 us
  Pallas kernels  50.9 us (95%)
  local copies, waits for them, and re-layouts  2.29 us (4%)
    pallas_call x1, Pallas kernels, local(): pl.pallas_call(fused_kernel, out_shape=jax.ShapeDtypeStruct(q_stream.shap...  50.9 us
    unnamed x1, local copies, waits for them, and re-layouts  2.29 us

profile of v4, /device:TPU:1, one launch (start us, length us, event | category | flops | bytes accessed | tf_op | source)
XLA Modules:
  0.0 53.2 jit_solution(3687882493815125171)
XLA Ops:
  0.0 50.9 %shard_map.136 = bf16[1,128,4096]{2,1,0:T(8,128)(2,1)} custom-call(s32[1,2]{1,0:T(1,128)} %lang_ref.1, f32[32,128]{1,0:T(8,128)} %bitcast.3, bf16[160,128]{1,0:T(8,128)(2,1)} %constant.10.clone.pick_ref, bf16[128,128]{1,0:T(8,128)(2,1)} %constant.11.clone.unpick_ref, bf16[1,128,4096]{2,1,0:T(8,128)(2,1)} %q_in.1, bf16[1,128,4096]{2,1,0:T(8,128)(2,1)} %k_in.1, ...), custom_call_target="tpu_custom_call" | custom-call | tf_op jit(solution)/shard_map/pallas_call | solution.py:506
  50.9 2.3 %copy.16 = bf16[1,128,4096]{2,1,0:T(8,128)(2,1)} copy(bf16[1,128,4096]{2,1,0:T(8,128)(2,1)} %shard_map.136) | data formatting | bytes 2097152

commit v5 on v4

--- a/solution.py
+++ b/solution.py
@@ -70,7 +70,7 @@
     return slice(b * LANES, (b + 1) * LANES)
 
 
-def stage_matmul(out_ref, left_ref, right_refs, width=512):
+def stage_matmul(out_ref, left_ref, right_refs, width=1024):
     columns = out_ref.shape[1]
 
     @pl.loop(0, columns // width)
@@ -136,7 +136,6 @@
 
 
 MESH = pl.DeviceIdType.MESH
-GROUP = 2
 
 
 def pick_tables():
@@ -192,11 +191,11 @@
 
 
 def fused_kernel(
-    lang_ref, skip_ref, pick_ref, unpick_ref, q_in, k_in, v_in, taps_in, down_in, up_in, filt_in, table_in,
+    lang_ref, skip_in, pick_in, unpick_in, q_in, k_in, v_in, taps_in, down_in, up_in, filt_in, table_in,
     back_in, step_in, out_ref,
     qv, kv, vv, qp, kp, vp, traw, tk_0, tk_1, tk_2, tk_3, tq_all, tsel, tqsel, down_all, up_all, down2, up2,
     halo32, halo_out, halo_in, send_x, recv_x, filt, table, back, step, high, low, p, h, tw, g, send_y, recv_y,
-    qs, gate, prod, out, back_sent, local_sem, halo_sem, tk_sem, tq_sem, down_sem, up_sem, x_send, x_recv, y_send, y_recv,
+    qs, gate, prod, out, back_sent, skip_ref, pick_ref, unpick_ref, local_sem, halo_sem, tk_sem, tq_sem, down_sem, up_sem, x_send, x_recv, y_send, y_recv,
     out_sem, line_sem, all_sem,
 ):
     y = lax.axis_index("lang")
@@ -209,10 +208,10 @@
             (taps_in, traw), (k_in.at[0], kv), (v_in.at[0], vv), (q_in.at[0], qv),
             (down_in, down_all.at[pl.ds(4 * y, 4)]), (up_in, up_all.at[pl.ds(4 * y, 4)]),
             (filt_in, filt), (table_in, table), (back_in, back), (step_in, step),
+            (skip_in, skip_ref), (unpick_in, unpick_ref), (pick_in, pick_ref),
         ])
     ]
-    for load in loads:
-        load.start()
+    loads[0].start()
 
     barrier = pltpu.get_barrier_semaphore()
     for r in range(1, 4):
@@ -220,6 +219,8 @@
     for r in (1, 2, 4, 6, 8, 16, 24):
         pl.semaphore_signal(barrier, inc=1, device_id={"seq": lax.bitwise_xor(me, r)}, device_id_type=MESH)
     pl.semaphore_signal(barrier, inc=1, device_id={"seq": lax.rem(me + 31, 32)}, device_id_type=MESH)
+    for load in loads[1:4] + loads[12:] + loads[4:12]:
+        load.start()
 
     def chip_of(i, j):
         return lax.bitwise_xor(lax.div(me, 2), 4 * j + lax.bitwise_xor(j, i))
@@ -273,6 +274,7 @@
         pos[pl.ds(0, 1), :] = halo32[pl.ds(2 * s, 1), :]
         pos[pl.ds(16, 1), :] = halo32[pl.ds(2 * s + 1, 1), :]
 
+    loads[12].wait()
     picked(kv, kp)
     picked(vv, vp)
     halo.wait_recv()
@@ -336,7 +338,7 @@
     picked(qv, qp)
     rimmed(2, qp)
 
-    for load in loads[6:]:
+    for load in loads[6:12]:
         load.wait()
     filter_spectrum(filt, table, step, high, low, p, h, tw)
     for n in range(16):
@@ -366,21 +368,21 @@
             device_id={"seq": d}, device_id_type=MESH,
         )
 
-    for i in range(0, 4, GROUP):
+    for i, group in ((0, 1), (1, 3)):
         @pl.loop(0, 2)
         def _(m, i=i):
             cols = columns(m, 512)
             both = jnp.concatenate([skip] * 4, 1)
             conv = jnp.dot(
-                back_sent[128 * i:128 * (i + GROUP), :], g[:, cols], preferred_element_type=jnp.float32
+                back_sent[128 * i:128 * (i + group), :], g[:, cols], preferred_element_type=jnp.float32
             )
-            for n in range(4 * GROUP):
+            for n in range(4 * group):
                 rows = pl.ds(pl.multiple_of(32 * chip_of(i + n // 4, n % 4), 32), 32)
                 send_y[128 * i + 32 * n:128 * i + 32 * n + 32, cols] = (
                     conv[32 * n:32 * n + 32] + both * recv_x[rows, cols].astype(jnp.float32)
                 ).astype(jnp.bfloat16)
 
-        @pl.loop(8 * i + (1 if i == 0 else 0), 8 * (i + GROUP))
+        @pl.loop(8 * i + (1 if i == 0 else 0), 8 * (i + group))
         def _(k):
             n, j, flip = lax.div(k, 8), lax.rem(lax.div(k, 2), 4), lax.rem(k, 2)
             y_copy(8 * j + 2 * lax.bitwise_xor(j, n) + flip).start()
@@ -433,32 +435,6 @@
 
     recv_y[me] = send_y[pl.ds(pl.multiple_of(core * 16, 16), 16), :]
 
-    def out_copy(i):
-        cols = columns(i, 256)
-        return pltpu.make_async_copy(out.at[:, cols], out_ref.at[0, :, cols], out_sem.at[i])
-
-    @pl.loop(0, 16)
-    def _(k):
-        n, j = lax.div(k, 4), lax.rem(k, 4)
-        r = 8 * j + 2 * lax.bitwise_xor(j, n)
-        chip = lax.bitwise_xor(lax.div(me, 2), lax.div(r, 2))
-        cols = columns(chip, 256)
-
-        @pl.when(k > 0)
-        def _():
-            y_copy(r).wait_recv()
-
-        y_copy(r + 1).wait_recv()
-        for one in range(2):
-            s = 2 * chip + one
-            for b in range(8):
-                piece = gate[pl.ds(b * 16, 16), columns(s)] * recv_y[s, :, lane(b)].astype(jnp.float32)
-                prod[pl.ds(b * 16, 16), lane(one)] = piece.astype(jnp.bfloat16)
-        out[:, cols] = jnp.dot(
-            unpick_ref[...], prod[...], preferred_element_type=jnp.float32
-        ).astype(jnp.bfloat16)
-        out_copy(chip).start()
-
     halo.wait_send()
     for get in chunks + [tq_get]:
         for r in (1, 2, 3):
@@ -475,7 +451,38 @@
     @pl.loop(1, 32)
     def _(r):
         x_copy(r).wait_send()
-        y_copy(r).wait_send()
+
+    def out_copy(i):
+        cols = columns(i, 256)
+        return pltpu.make_async_copy(out.at[:, cols], out_ref.at[0, :, cols], out_sem.at[i])
+
+    @pl.loop(0, 16)
+    def _(k):
+        n, j = lax.div(k, 4), lax.rem(k, 4)
+        r = 8 * j + 2 * lax.bitwise_xor(j, n)
+        chip = lax.bitwise_xor(lax.div(me, 2), lax.div(r, 2))
+        cols = columns(chip, 256)
+
+        @pl.when(k > 0)
+        def _():
+            y_copy(r).wait_recv()
+
+        y_copy(r + 1).wait_recv()
+        for one in range(2):
+            s = 2 * chip + one
+            for b in range(8):
+                piece = gate[pl.ds(b * 16, 16), columns(s)] * recv_y[s, :, lane(b)].astype(jnp.float32)
+                prod[pl.ds(b * 16, 16), lane(one)] = piece.astype(jnp.bfloat16)
+        out[:, cols] = jnp.dot(
+            unpick_ref[...], prod[...], preferred_element_type=jnp.float32
+        ).astype(jnp.bfloat16)
+        out_copy(chip).start()
+
+        @pl.when(k > 0)
+        def _():
+            y_copy(r).wait_send()
+
+        y_copy(r + 1).wait_send()
 
     @pl.loop(0, 16)
     def _(i):
@@ -486,7 +493,6 @@
     fwd, back, step = dft_tables()
     pick, unpick = pick_tables()
     bf16, f32 = jnp.bfloat16, jnp.float32
-    vmem = pl.BlockSpec(memory_space=pltpu.VMEM)
     anywhere = pl.BlockSpec(memory_space=pl.ANY)
     dma = pltpu.SemaphoreType.DMA
     arrays = [
@@ -502,14 +508,15 @@
         ((1024, 1024), f32), ((1024, 1024), f32), ((1024, 1024), f32), ((1024, 1024), bf16),
         ((512, 1024), bf16), ((32, 16, 1024), bf16),
         ((128, 4096), bf16), ((128, 4096), f32), ((128, 256), bf16), ((128, 4096), bf16), ((512, 1024), bf16),
+        ((32, 128), f32), ((160, 128), bf16), ((128, 128), bf16),
     ]
     return pl.pallas_call(
         fused_kernel,
         out_shape=jax.ShapeDtypeStruct(q_stream.shape, bf16),
-        in_specs=[pl.BlockSpec(memory_space=pltpu.SMEM)] + [vmem] * 3 + [anywhere] * 10,
+        in_specs=[pl.BlockSpec(memory_space=pltpu.SMEM)] + [anywhere] * 13,
         out_specs=anywhere,
         scratch_shapes=[pltpu.VMEM(shape, kind) for shape, kind in arrays]
-        + [dma((10,)), dma((2,)), dma((4, 4, 3)), dma((4, 3)), dma((4, 3)), dma((4, 3))]
+        + [dma((13,)), dma((2,)), dma((4, 4, 3)), dma((4, 3)), dma((4, 3)), dma((4, 3))]
         + [dma((32,))] * 4
         + [dma((16,)), pltpu.SemaphoreType.REGULAR, pltpu.SemaphoreType.REGULAR],
         compiler_params=pltpu.CompilerParams(

time: 53.4 us -> 53 us (level)
  no operation moved by 1% of the time
where the time goes in v5:
time: 53 us; the launch traced here: 52.9 us
  Pallas kernels  50.6 us (95%)
  local copies, waits for them, and re-layouts  2.29 us (4%)
    pallas_call x1, Pallas kernels, local(): pl.pallas_call(fused_kernel, out_shape=jax.ShapeDtypeStruct(q_stream.shap...  50.6 us
    unnamed x1, local copies, waits for them, and re-layouts  2.29 us

profile of v5, /device:TPU:1, one launch (start us, length us, event | category | flops | bytes accessed | tf_op | source)
XLA Modules:
  0.0 52.9 jit_solution(1716014337876880)
XLA Ops:
  0.0 50.6 %shard_map.136 = bf16[1,128,4096]{2,1,0:T(8,128)(2,1)} custom-call(s32[1,2]{1,0:T(1,128)} %lang_ref.1, f32[32,128]{1,0:T(8,128)} %bitcast.3, bf16[160,128]{1,0:T(8,128)(2,1)} %constant.10.clone.pick_in, bf16[128,128]{1,0:T(8,128)(2,1)} %constant.11.clone.unpick_in, bf16[1,128,4096]{2,1,0:T(8,128)(2,1)} %q_in.1, bf16[1,128,4096]{2,1,0:T(8,128)(2,1)} %k_in.1, ...), custom_call_target="tpu_custom_call" | custom-call | tf_op jit(solution)/shard_map/pallas_call | solution.py:513
  50.6 2.3 %copy.16 = bf16[1,128,4096]{2,1,0:T(8,128)(2,1)} copy(bf16[1,128,4096]{2,1,0:T(8,128)(2,1)} %shard_map.136) | data formatting | bytes 2097152

commit v6 on v5

--- a/solution.py
+++ b/solution.py
@@ -369,10 +369,10 @@
         )
 
     for i, group in ((0, 1), (1, 3)):
-        @pl.loop(0, 2)
+        @pl.loop(0, 1)
         def _(m, i=i):
-            cols = columns(m, 512)
-            both = jnp.concatenate([skip] * 4, 1)
+            cols = columns(m, 1024)
+            both = jnp.concatenate([skip] * 8, 1)
             conv = jnp.dot(
                 back_sent[128 * i:128 * (i + group), :], g[:, cols], preferred_element_type=jnp.float32
             )

time: 53 us -> 52.9 us (level)
  no operation moved by 1% of the time
where the time goes in v6:
time: 52.9 us; the launch traced here: 52.7 us
  Pallas kernels  50.5 us (95%)
  local copies, waits for them, and re-layouts  2.29 us (4%)
    pallas_call x1, Pallas kernels, local(): pl.pallas_call(fused_kernel, out_shape=jax.ShapeDtypeStruct(q_stream.shap...  50.5 us
    unnamed x1, local copies, waits for them, and re-layouts  2.29 us

profile of v6, /device:TPU:1, one launch (start us, length us, event | category | flops | bytes accessed | tf_op | source)
XLA Modules:
  0.0 52.7 jit_solution(7887479925495692961)
XLA Ops:
  0.0 50.5 %shard_map.136 = bf16[1,128,4096]{2,1,0:T(8,128)(2,1)} custom-call(s32[1,2]{1,0:T(1,128)} %lang_ref.1, f32[32,128]{1,0:T(8,128)} %bitcast.3, bf16[160,128]{1,0:T(8,128)(2,1)} %constant.10.clone.pick_in, bf16[128,128]{1,0:T(8,128)(2,1)} %constant.11.clone.unpick_in, bf16[1,128,4096]{2,1,0:T(8,128)(2,1)} %q_in.1, bf16[1,128,4096]{2,1,0:T(8,128)(2,1)} %k_in.1, ...), custom_call_target="tpu_custom_call" | custom-call | tf_op jit(solution)/shard_map/pallas_call | solution.py:513
  50.5 2.3 %copy.16 = bf16[1,128,4096]{2,1,0:T(8,128)(2,1)} copy(bf16[1,128,4096]{2,1,0:T(8,128)(2,1)} %shard_map.136) | data formatting | bytes 2097152

commit v7 on v6

--- a/solution.py
+++ b/solution.py
@@ -368,7 +368,7 @@
             device_id={"seq": d}, device_id_type=MESH,
         )
 
-    for i, group in ((0, 1), (1, 3)):
+    for i, group in ((0, 2), (2, 2)):
         @pl.loop(0, 1)
         def _(m, i=i):
             cols = columns(m, 1024)

time: 52.9 us -> 52.9 us (level)
  no operation moved by 1% of the time
where the time goes in v7:
time: 52.9 us; the launch traced here: 52.8 us
  Pallas kernels  50.5 us (95%)
  local copies, waits for them, and re-layouts  2.29 us (4%)
    pallas_call x1, Pallas kernels, local(): pl.pallas_call(fused_kernel, out_shape=jax.ShapeDtypeStruct(q_stream.shap...  50.5 us
    unnamed x1, local copies, waits for them, and re-layouts  2.29 us

profile of v7, /device:TPU:1, one launch (start us, length us, event | category | flops | bytes accessed | tf_op | source)
XLA Modules:
  0.0 52.8 jit_solution(13239732656663121245)
XLA Ops:
  0.0 50.5 %shard_map.136 = bf16[1,128,4096]{2,1,0:T(8,128)(2,1)} custom-call(s32[1,2]{1,0:T(1,128)} %lang_ref.1, f32[32,128]{1,0:T(8,128)} %bitcast.3, bf16[160,128]{1,0:T(8,128)(2,1)} %constant.10.clone.pick_in, bf16[128,128]{1,0:T(8,128)(2,1)} %constant.11.clone.unpick_in, bf16[1,128,4096]{2,1,0:T(8,128)(2,1)} %q_in.1, bf16[1,128,4096]{2,1,0:T(8,128)(2,1)} %k_in.1, ...), custom_call_target="tpu_custom_call" | custom-call | tf_op jit(solution)/shard_map/pallas_call | solution.py:513
  50.5 2.3 %copy.16 = bf16[1,128,4096]{2,1,0:T(8,128)(2,1)} copy(bf16[1,128,4096]{2,1,0:T(8,128)(2,1)} %shard_map.136) | data formatting | bytes 2097152
